TPU v7x, 512 devices: a whole 4x8x8 slice. The times are simulated.
512 devices in a mesh: period: 16 (over z, core), block: 32 (over y, x).
Axes of the slice: x: 4, y: 8, z: 8, core: 2. Of those that a mesh axis runs over, the one named last changes fastest.
Arguments:
- link_rows: bfloat16 [1048576, 512], P(('period', 'block')), may hold values from -1.5 to 1.5
- barrier_weights: float32 [1048576], P(('period', 'block')), may hold values from 0.1 to 10
- row_residual: float32 [1048576], P(('period', 'block')), may hold values from -6 to 6
- tile_pattern: int32 [8192, 4], P(('period', 'block')), may hold values 0 or 1
- block_rows: int32 [512], P(('period', 'block')), may hold values from 1 to 2048, 349525 in all
- link_diag: float32 [512], replicated, may hold values from 0.05 to 0.5
Outputs:
- row_step: float32 [1048576], P(('period', 'block'))
- link_step: float32 [512], replicated
Inputs may be any that keep to these rules, and one draw needn't show every extreme that they name: `block_rows`: each block has between 1 and 2048 live rows; some block has exactly 2048.
All inputs are finite; a program needn't handle non-finite values. No bound on the sum of `tile_pattern` on one device may be relied on, other than what follows from the above.
Results may differ from a plain program's by a relative error of at most 0.0055.
The roundings to bfloat16 on the way count: a program that leaves them out, or rounds other values in their place, can miss the bound.
Values sent between devices are 32-bit elements; how exact they have to be, the bound alone decides.
No kernel may reach another device: no remote copies, remote signals or barrier semaphores. Data moves between devices by JAX's collectives and lax.ppermute only.
A program may use at most 64 MiB of HBM per device.

v0:
```python
import jax
import jax.numpy as jnp
from jax import lax
from jax.sharding import PartitionSpec as P

TILE = 128


def on_device(link_rows, barrier_weights, row_residual, tile_pattern, block_rows, link_diag):
    row_count = link_rows.shape[0]
    width = link_rows.shape[1]
    count = block_rows[0]
    live = (jnp.arange(row_count) < count).astype(jnp.float32)
    cover = jnp.repeat(jnp.repeat(tile_pattern, TILE, axis=0), TILE, axis=1).astype(jnp.float32)
    masked = link_rows * (cover * live[:, None]).astype(jnp.bfloat16)
    scaled = (masked.astype(jnp.float32) * jnp.sqrt(barrier_weights)[:, None]).astype(jnp.bfloat16)
    weighted = (barrier_weights * row_residual * live).astype(jnp.bfloat16)
    tile_count = (count + TILE - 1) // TILE

    def add_tile(index, total):
        first = index * TILE
        piece = lax.dynamic_slice_in_dim(scaled, first, TILE, 0)
        return total + lax.dot_general(
            piece, piece, (((0,), (0,)), ((), ())), preferred_element_type=jnp.float32
        )

    contrib = lax.fori_loop(0, tile_count, add_tile, jnp.zeros((width, width), jnp.float32))
    partial_value = lax.dot_general(
        masked, weighted, (((0,), (0,)), ((), ())), preferred_element_type=jnp.float32
    )
    matrix, vector = (contrib, partial_value)
    matrix, vector = lax.psum((matrix, vector), ("period", "block"))
    schur, gradient = (matrix, vector)
    schur = schur + jnp.diag(link_diag)
    factor = jnp.linalg.cholesky(schur)
    link_step = jax.scipy.linalg.cho_solve((factor, True), gradient)
    step_b = link_step.astype(jnp.bfloat16)
    moved = jnp.dot(masked, step_b, preferred_element_type=jnp.float32)
    row_step = live * barrier_weights * (moved - row_residual)
    return (row_step, link_step)


def solution(mesh):
    return jax.shard_map(
        on_device,
        mesh=mesh,
        in_specs=(
            P(("period", "block"), None),
            P(("period", "block")),
            P(("period", "block")),
            P(("period", "block"), None),
            P(("period", "block")),
            P(),
        ),
        out_specs=(P(("period", "block")), P()),
        check_vma=False,
    )
```

profile of v0, /device:TPU:1, one launch (start us, length us, event | category | flops | bytes accessed | tf_op | source)
XLA Modules:
  0.0 485.6 jit_solution(11479640656240418069)
XLA Ops:
  9.5 4.7 broadcast_in_dim.32
  14.1 1.9 multiply_convert_fusion
  16.2 9.3 %while.11 = (s32[]{:T(128)}, f32[512,512]{1,0:T(8,128)S(1)}, s32[]{:T(128)}, bf16[2048,512]{1,0:T(8,128)(2,1)}, s32[]{:T(128)}, /*index=5*/s32[]{:T(128)}, s32[]{:T(128)}, s32[]{:T(128)}) while((s32[]{:T(128)}, f32[512,512]{1,0:T(8,128)S(1)}, s32[]{:T(128)}, bf16[2048,512]{1,0:T(8,128)(2,1)}, s32[]{:T(128)}, /*index=5*/s32[]{:T(128)}, ...), condition=%wide.region_1.2_spmd, body=%wide.region_0.1_spmd.sunk | while | flops 67371016 | bytes 2228367 | solution.py:27
  25.5 1.4 copy.10
  27.3 118.5 %psum.15 = f32[512]{0:T(512)S(1)} all-reduce(f32[512]{0:T(512)S(1)} %bitcast.161), channel_id=1, replica_groups=mesh['period'=16,'block'=32] {'period','block'}, use_global_device_ids=true, to_apply=%region_11.12 | all-reduce | flops 512 | bytes 4096 | tf_op jit(solution)/shard_map/psum | solution.py:32
  145.8 173.4 %all-reduce.3.cloned.1.call-done = f32[512,512]{0,1:T(8,128)} async-done(((f32[512,512]{0,1:T(8,128)}), f32[512,512]{0,1:T(8,128)}) %all-reduce.3.cloned.1.call-update) | async-done | bytes 1048592 | tf_op jit(solution)/shard_map/psum | solution.py:32
  319.2 1.3 select_add_fusion
  320.5 1.4 copy.11
  321.9 1.8 fusion.16
  323.7 11.7 %cholesky.103 = f32[128,128]{1,0:T(8,128)S(1)} custom-call(f32[128,128]{1,0:T(8,128)S(1)} %cholesky.263), custom_call_target="Cholesky" | custom-call | tf_op jit(solution)/shard_map/jit(cholesky)/cholesky | solution.py:35
  336.2 9.8 %custom-call.34 = f32[1,128,128]{1,2,0:T(8,128)S(1)} custom-call(f32[1,128,128]{2,1,0:T(8,128)S(1)} %get-tuple-element.67), custom_call_target="InvertDiagBlocksLowerTriangular" | custom-call | tf_op jit(solution)/shard_map/jit(cholesky)/cholesky | solution.py:35
  347.5 11.7 %cholesky.215 = f32[128,128]{1,0:T(8,128)S(1)} custom-call(f32[128,128]{1,0:T(8,128)S(1)} %cholesky.267), custom_call_target="Cholesky" | custom-call | tf_op jit(solution)/shard_map/jit(cholesky)/cholesky | solution.py:35
  360.3 10.0 %custom-call.35 = f32[1,128,128]{1,2,0:T(8,128)S(1)} custom-call(f32[1,128,128]{2,1,0:T(8,128)S(1)} %get-tuple-element.65), custom_call_target="InvertDiagBlocksLowerTriangular" | custom-call | tf_op jit(solution)/shard_map/jit(cholesky)/cholesky | solution.py:35
  371.6 1.5 convolution_subtract_fusion.1
  373.1 11.7 %cholesky.236 = f32[128,128]{1,0:T(8,128)S(1)} custom-call(f32[128,128]{1,0:T(8,128)S(1)} %cholesky.272), custom_call_target="Cholesky" | custom-call | tf_op jit(solution)/shard_map/jit(cholesky)/cholesky | solution.py:35
  384.9 9.8 %custom-call.36 = f32[1,128,128]{1,2,0:T(8,128)S(1)} custom-call(f32[1,128,128]{2,1,0:T(8,128)S(1)} %get-tuple-element.63), custom_call_target="InvertDiagBlocksLowerTriangular" | custom-call | tf_op jit(solution)/shard_map/jit(cholesky)/cholesky | solution.py:35
  395.1 1.3 convolution_subtract_fusion.2
  396.4 11.9 %cholesky.253 = f32[128,128]{1,0:T(8,128)S(1)} custom-call(f32[128,128]{1,0:T(8,128)S(1)} %convolution_subtract_fusion.2), custom_call_target="Cholesky" | custom-call | tf_op jit(solution)/shard_map/jit(cholesky)/cholesky | solution.py:35
  414.1 14.9 %while.12 = (s32[]{:T(128)}, f32[512,512]{0,1:T(8,128)}, s32[4,2]{0,1:T(2,128)S(1)}, f32[4,128,128]{2,1,0:T(8,128)}, s32[]{:T(128)}) while((s32[]{:T(128)}, f32[512,512]{0,1:T(8,128)}, s32[4,2]{0,1:T(2,128)S(1)}, f32[4,128,128]{2,1,0:T(8,128)}, s32[]{:T(128)}) %tuple.47), condition=%wide.while_cond, body=%wide.while_body.sunk | while | flops 2 | bytes 393329 | solution.py:36
  414.8 2.3 dynamic-slice.7
  418.5 2.3 dynamic-slice.7
  422.3 2.3 dynamic-slice.7
  426.0 2.3 dynamic-slice.7
  429.0 40.1 %custom-call.37 = f32[4,128,128]{1,2,0:T(8,128)S(1)} custom-call(f32[4,128,128]{2,1,0:T(8,128)} %get-tuple-element.33), custom_call_target="InvertDiagBlocksLowerTriangular" | custom-call | tf_op jit(solution)/shard_map/jit(_cho_solve)/triangular_solve | solution.py:36
  (94 shorter events, 34.6 us)
Async XLA Ops:
  7.2 312.0 %all-reduce.3.cloned.1.call-start = ((), (), s32[]{:S(2)}) async-start(), calls=%async_computation | async-start | bytes 2097152 | tf_op jit(solution)/shard_map/psum | solution.py:32
  9.4 4.7 copy-start.1
  26.9 292.3 %copy-start.6 = (f32[512]{0:T(512)S(1)}, f32[512]{0:T(512)}, u32[]{:S(2)}) copy-start(f32[512]{0:T(512)} %param.13) | copy-start | bytes 6148
  323.7 35.6 %copy-start = (f32[512,512]{1,0:T(8,128)}, f32[512,512]{1,0:T(8,128)S(1)}, u32[]{:S(2)}) copy-start(f32[512,512]{1,0:T(8,128)S(1)} %fusion.16) | copy-start | bytes 3145732
  346.8 0.7 copy-start.2
  429.0 49.1 %copy-start.3 = (f32[2048]{0:T(1024)S(1)}, f32[2048]{0:T(1024)}, u32[]{:S(2)}) copy-start(f32[2048]{0:T(1024)} %param.9) | copy-start | bytes 24580
  429.0 49.1 %copy-start.4 = (f32[2048]{0:T(1024)S(1)}, f32[2048]{0:T(1024)}, u32[]{:S(2)}) copy-start(f32[2048]{0:T(1024)} %param.10) | copy-start | bytes 24580
  477.4 1.3 copy-start.5
Sparse Core Ops, SparseCore 0:
  27.0 292.1 all-reduce.2
where the time goes:
time: 488 us; the launch traced here: 486 us
  waiting for transfers between devices  173 us (35%)
  other arithmetic  127 us (26%)
  blocking collectives  118 us (24%)
  local copies, waits for them, and re-layouts  25.4 us (5%)
  matrix products  23.3 us (5%)
  between operations  17.5 us (4%)
    psum x1, waiting for transfers between devices, on_device(): matrix, vector = lax.psum((matrix, vector), ('period', 'block'))  173 us
    psum x1, blocking collectives, on_device(): matrix, vector = lax.psum((matrix, vector), ('period', 'block'))  118 us
    another operation x14, other arithmetic, on_device(): factor = jnp.linalg.cholesky(schur)  78.8 us
    another operation x4, other arithmetic, on_device(): link_step = jax.scipy.linalg.cho_solve((factor, True), gradient)  41.3 us
    another operation x20, local copies, waits for them, and re-layouts  14.8 us
  transfers between devices with their start and end apart: 1, of which 1 were waited for; matrix products, arithmetic and copies ran while one was open for 0% of the time, Pallas kernels for 0%

commit v1 on v0

v1 whole, which is shorter than its diff:
```python
import functools

import jax
import jax.numpy as jnp
from jax import lax
from jax.experimental import pallas as pl
from jax.experimental.pallas import tpu as pltpu
from jax.sharding import Mesh, PartitionSpec as P

TILE = 128
WIDTH = 512
ROWS = 2048
TILES = ROWS // TILE
CHUNKS = 4
F32 = jnp.float32
BF16 = jnp.bfloat16
HIGH = lax.Precision.HIGHEST
HALF = 544
NAMES = ("z", "core", "y", "x")


def iota(shape, axis):
    return lax.broadcasted_iota(jnp.int32, shape, axis)


def dot_nn(a, b):
    return lax.dot_general(a, b, (((1,), (0,)), ((), ())), precision=HIGH, preferred_element_type=F32)


def dot_nt(a, b):
    return lax.dot_general(a, b, (((1,), (1,)), ((), ())), precision=HIGH, preferred_element_type=F32)


def assemble_kernel(count_ref, pattern_ref, rows_hbm, weights_ref, resid_ref, out_ref, rows, scaled, sems):
    step = ROWS // CHUNKS
    copies = [
        pltpu.make_async_copy(rows_hbm.at[pl.ds(i * step, step)], rows.at[pl.ds(i * step, step)], sems.at[i])
        for i in range(CHUNKS)
    ]
    for copy in copies:
        copy.start()
    count = count_ref[0]
    shape = (TILES, TILE)
    live = (iota(shape, 0) * TILE + iota(shape, 1) < count).astype(F32)
    weights = weights_ref[...]
    root = jnp.sqrt(weights) * live
    weighted = (weights * resid_ref[...] * live).astype(BF16).astype(F32)
    columns = jnp.concatenate([root, weighted, jnp.zeros((TILE - 2 * TILES, TILE), F32)], axis=0).T
    gradient = [jnp.zeros((8, TILE), F32) for _ in range(4)]
    for t in range(TILES):
        if t % (TILES // CHUNKS) == 0:
            copies[t // (TILES // CHUNKS)].wait()
        root_t = jnp.broadcast_to(columns[:, t : t + 1], (TILE, TILE))
        weighted_t = jnp.broadcast_to(columns[:, TILES + t : TILES + t + 1], (TILE, TILE))
        for j in range(4):
            cover = pattern_ref[t, j].astype(F32)
            x = rows[pl.ds(t * TILE, TILE), pl.ds(j * TILE, TILE)].astype(F32) * cover
            scaled[pl.ds(t * TILE, TILE), pl.ds(j * TILE, TILE)] = (x * root_t).astype(BF16)
            gradient[j] = gradient[j] + jnp.sum((x * weighted_t).reshape(TILE // 8, 8, TILE), axis=0)
    below = iota((TILE, TILE), 0) >= iota((TILE, TILE), 1)
    same = iota((TILE, TILE), 0) == iota((TILE, TILE), 1)

    def gram(i, j):
        return lax.dot_general(
            scaled[:, pl.ds(i * 256, 256)],
            scaled[:, pl.ds(j * 256, 256)],
            (((0,), (0,)), ((), ())),
            preferred_element_type=F32,
        )

    def finish(base, block, corner, pieces, first):
        a, b = block[:TILE, :TILE], block[TILE:, TILE:]
        out_ref[pl.ds(base, TILE), :] = jnp.where(below, a, b)
        out_ref[pl.ds(base + TILE, TILE), :] = corner
        for i, piece in enumerate(pieces):
            out_ref[pl.ds(base + (2 + i) * TILE, TILE), :] = piece
        diagonal = jnp.sum(jnp.where(same, b, 0.0), axis=0, keepdims=True)
        parts = [jnp.sum(gradient[first], axis=0, keepdims=True), jnp.sum(gradient[first + 1], axis=0, keepdims=True), diagonal]
        out_ref[pl.ds(base + 4 * TILE, 8), :] = jnp.concatenate(parts + [jnp.zeros((5, TILE), F32)], axis=0)
        out_ref[pl.ds(base + 4 * TILE + 8, 24), :] = jnp.zeros((24, TILE), F32)

    top, low, cross = gram(0, 0), gram(1, 1), gram(1, 0)
    finish(0, top, top[TILE:, :TILE], (cross[:TILE, :TILE], cross[TILE:, :TILE]), 0)
    finish(HALF, low, low[TILE:, :TILE], (cross[:TILE, TILE:], cross[TILE:, TILE:]), 2)


def assemble(count, pattern, rows, weights, resid):
    vmem = pl.BlockSpec(memory_space=pltpu.VMEM)
    smem = pl.BlockSpec(memory_space=pltpu.SMEM)
    return pl.pallas_call(
        assemble_kernel,
        out_shape=jax.ShapeDtypeStruct((2 * HALF, TILE), F32),
        in_specs=[smem, smem, pl.BlockSpec(memory_space=pl.ANY), vmem, vmem],
        out_specs=vmem,
        scratch_shapes=[
            pltpu.VMEM((ROWS, WIDTH), BF16),
            pltpu.VMEM((ROWS, WIDTH), BF16),
            pltpu.SemaphoreType.DMA((CHUNKS,)),
        ],
        name="assemble",
    )(count, pattern, rows, weights, resid)


def invert(block):
    groups = [block[8 * i : 8 * i + 8, :] for i in range(16)]
    lane, sub = iota((8, TILE), 1), iota((8, TILE), 0)
    wide = lambda v: jnp.broadcast_to(v, (8, TILE))
    for k in range(16):
        split = [[wide(g[:, 8 * k + j : 8 * k + j + 1]) for j in range(8)] for g in groups]
        inside = (lane >= 8 * k) & (lane < 8 * k + 8)
        panel = jnp.where(inside, (lane - 8 * k == sub).astype(F32), groups[k])
        cols = list(split[k])
        for j in range(8):
            here = sub == j
            inverse = 1.0 / wide(cols[j][j : j + 1, :])
            pivot = cols[j]
            scaled_row = wide(panel[j : j + 1, :]) * inverse
            panel = jnp.where(here, scaled_row, panel - pivot * scaled_row)
            for c in range(j + 1, 8):
                entry = wide(cols[c][j : j + 1, :]) * inverse
                cols[c] = jnp.where(here, entry, cols[c] - pivot * entry)
        spread = [wide(panel[j : j + 1, :]) for j in range(8)]
        for i in range(16):
            if i != k:
                terms = [split[i][j] * spread[j] for j in range(8)]
                total = ((terms[0] + terms[1]) + (terms[2] + terms[3])) + ((terms[4] + terms[5]) + (terms[6] + terms[7]))
                groups[i] = jnp.where(inside, 0.0, groups[i]) - total
        groups[k] = panel
    return jnp.concatenate(groups, axis=0)


def solve_kernel(
    count_ref, rows_hbm, packed_ref, diag_ref, weights_ref, resid_ref, pattern_ref, row_step_ref, step_ref,
    rows, matrix, inverses, sem,
):
    copy = pltpu.make_async_copy(rows_hbm, rows, sem)
    copy.start()
    below = iota((TILE, TILE), 0) >= iota((TILE, TILE), 1)
    same = iota((TILE, TILE), 0) == iota((TILE, TILE), 1)
    link = diag_ref[...]

    def tile(i, j):
        return pl.ds(i * TILE, TILE), pl.ds(j * TILE, TILE)

    gradient = []
    for h in range(2):
        base = h * HALF
        folded = packed_ref[pl.ds(base, TILE), :]
        turned = folded.T
        extras = packed_ref[pl.ds(base + 4 * TILE, 8), :]
        gradient += [extras[0:1], extras[1:2]]
        i = 2 * h
        matrix[tile(i, i)] = jnp.where(below, folded, turned) + jnp.where(same, link[i : i + 1, :], 0.0)
        matrix[tile(i + 1, i + 1)] = jnp.where(same, extras[2:3] + link[i + 1 : i + 2, :], jnp.where(below, turned, folded))
        matrix[tile(i + 1, i)] = packed_ref[pl.ds(base + TILE, TILE), :]
        matrix[tile(2, h)] = packed_ref[pl.ds(base + 2 * TILE, TILE), :]
        matrix[tile(3, h)] = packed_ref[pl.ds(base + 3 * TILE, TILE), :]
    factors = {}
    for k in range(4):
        inverse = invert(matrix[tile(k, k)])
        inverses[k] = inverse
        for i in range(k + 1, 4):
            factors[i, k] = dot_nn(matrix[tile(i, k)], inverse)
        for i in range(k + 1, 4):
            gradient[i] = gradient[i] - dot_nt(gradient[k], factors[i, k])
            for j in range(k + 1, i + 1):
                matrix[tile(i, j)] = matrix[tile(i, j)] - dot_nt(factors[i, k], matrix[tile(j, k)])
    steps = [None] * 4
    for k in reversed(range(4)):
        value = dot_nn(gradient[k], inverses[k])
        for i in range(k + 1, 4):
            value = value - dot_nn(steps[i], factors[i, k])
        steps[k] = value
    step_ref[...] = jnp.concatenate(steps, axis=0)
    copy.wait()
    rounded = [jnp.broadcast_to(v, (TILES, TILE)) for v in steps]
    present = pattern_ref[...].astype(F32)
    left = jnp.concatenate(
        [v * jnp.broadcast_to(present[:, j : j + 1], (TILES, TILE)) for j, v in enumerate(rounded)], axis=1
    ).astype(BF16)
    shape = (TILES, TILE)
    moved = jnp.zeros(shape, F32)
    for t in range(TILES):
        part = lax.dot_general(
            left, rows[pl.ds(t * TILE, TILE), :], (((1,), (1,)), ((), ())), preferred_element_type=F32
        )
        moved = jnp.where(iota(shape, 0) == t, part, moved)
    live = (iota(shape, 0) * TILE + iota(shape, 1) < count_ref[0]).astype(F32)
    row_step_ref[...] = live * weights_ref[...] * (moved - resid_ref[...])


def solve(count, rows, packed, diag, weights, resid, pattern):
    vmem = pl.BlockSpec(memory_space=pltpu.VMEM)
    smem = pl.BlockSpec(memory_space=pltpu.SMEM)
    return pl.pallas_call(
        solve_kernel,
        out_shape=(jax.ShapeDtypeStruct((TILES, TILE), F32), jax.ShapeDtypeStruct((4, TILE), F32)),
        in_specs=[smem, pl.BlockSpec(memory_space=pl.ANY), vmem, vmem, vmem, vmem, vmem],
        out_specs=(vmem, vmem),
        scratch_shapes=[
            pltpu.VMEM((ROWS, WIDTH), BF16),
            pltpu.VMEM((WIDTH, WIDTH), F32),
            pltpu.VMEM((4, TILE, TILE), F32),
            pltpu.SemaphoreType.DMA,
        ],
        name="solve",
    )(count, rows, packed, diag, weights, resid, pattern)


def exchange(x, axes):
    return lax.all_to_all(x, axes, split_axis=0, concat_axis=0, tiled=True)


def reduce_all(packed):
    core = lax.axis_index("core")
    keep = lax.dynamic_slice_in_dim(packed, core * HALF, HALF, 0)
    give = lax.dynamic_slice_in_dim(packed, (1 - core) * HALF, HALF, 0)
    swap = [(0, 1), (1, 0)]
    half = keep + lax.ppermute(give, "core", swap)
    pieces = exchange(half.reshape(32, 17, TILE), ("y", "x"))
    piece = jnp.sum(pieces, axis=0)
    layers = exchange(jnp.broadcast_to(piece[None], (8, 17, TILE)), "z")
    piece = jnp.sum(layers, axis=0)
    half = exchange(jnp.broadcast_to(piece[None], (32, 17, TILE)), ("y", "x")).reshape(HALF, TILE)
    other = lax.ppermute(half, "core", swap)
    return jnp.where(core == 0, jnp.concatenate([half, other]), jnp.concatenate([other, half]))


def on_device(link_rows, barrier_weights, row_residual, tile_pattern, block_rows, link_diag):
    weights = barrier_weights.reshape(TILES, TILE)
    resid = row_residual.reshape(TILES, TILE)
    packed = assemble(block_rows, tile_pattern, link_rows, weights, resid)
    packed = reduce_all(packed)
    row_step, step = solve(block_rows, link_rows, packed, link_diag.reshape(4, TILE), weights, resid, tile_pattern)
    return row_step.reshape(ROWS), step.reshape(WIDTH)


def solution(mesh):
    fine = Mesh(mesh.devices.reshape(8, 2, 8, 4), NAMES)
    return jax.shard_map(
        on_device,
        mesh=fine,
        in_specs=(P(NAMES, None), P(NAMES), P(NAMES), P(NAMES, None), P(NAMES), P()),
        out_specs=(P(NAMES), P()),
        check_vma=False,
    )
```

time: 488 us -> 111 us (0.23)
  waiting for transfers between devices: 173 us -> 2.14 us
  other arithmetic: 127 us -> 1.86 us
  blocking collectives: 118 us -> 51.8 us
  Pallas kernels: 0 us -> 34.8 us
  matrix products: 23.3 us -> 0 us
  local copies, waits for them, and re-layouts: 25.4 us -> 2.42 us
  starting transfers between devices: 0.04 us -> 16.1 us
  between operations: 17.5 us -> 1.54 us
    psum x1 -> x0, waiting for transfers between devices: 173 us -> none  [on_device(): matrix, vector = lax.psum((matrix, vector), ('period', 'block'))]
    another operation x18 -> x0, other arithmetic: 120 us -> none  [the longest x14 78.8 us: on_device(): factor = jnp.linalg.cholesky(schur)]
    psum x1 -> x0, blocking collectives: 118 us -> none  [on_device(): matrix, vector = lax.psum((matrix, vector), ('period', 'block'))]
    all_to_all x0 -> x3, blocking collectives: none -> 51.8 us  [exchange(): return lax.all_to_all(x, axes, split_axis=0, concat_axis=0, tiled=True)]
    pallas_call x0 -> x2, Pallas kernels: none -> 34.8 us  [the longest x1 30.1 us: solve(): pl.pallas_call(solve_kernel, out_shape=(jax.ShapeDtypeStruct((TILES, TILE...]
    another operation x34 -> x0, local copies, waits for them, and re-layouts: 17 us -> none
    ppermute x0 -> x2, starting transfers between devices: none -> 16.1 us  [the longest x1 8.75 us: reduce_all(): half = keep + lax.ppermute(give, 'core', swap)]
    another operation x20 -> x0, matrix products: 13.2 us -> none  [the longest x14 8.23 us: on_device(): link_step = jax.scipy.linalg.cho_solve((factor, True), gradient)]
  transfers between devices with their start and end apart: 1 -> 2, of which waited for: 1 -> 2; matrix products, arithmetic and copies ran while one was open for 0% -> 0% of each run, Pallas kernels for 0% -> 0%
where the time goes in v1:
time: 111 us
  blocking collectives  51.8 us (47%)
  Pallas kernels  34.8 us (31%)
  starting transfers between devices  16.1 us (15%)
  local copies, waits for them, and re-layouts  2.42 us (2%)
  waiting for transfers between devices  2.14 us (2%)
  other arithmetic  1.86 us (2%)
  between operations  1.54 us (1%)
    all_to_all x3, blocking collectives, exchange(): return lax.all_to_all(x, axes, split_axis=0, concat_axis=0, tiled=True)  51.8 us
    pallas_call x1, Pallas kernels, solve(): pl.pallas_call(solve_kernel, out_shape=(jax.ShapeDtypeStruct((TILES, TILE...  30.1 us
    ppermute x1, starting transfers between devices, reduce_all(): half = keep + lax.ppermute(give, 'core', swap)  8.75 us
    ppermute x1, starting transfers between devices, reduce_all(): other = lax.ppermute(half, 'core', swap)  7.38 us
    pallas_call x1, Pallas kernels, assemble(): pl.pallas_call(assemble_kernel, out_shape=jax.ShapeDtypeStruct((2 * HALF,...  4.61 us
  transfers between devices with their start and end apart: 2, of which 2 were waited for; matrix products, arithmetic and copies ran while one was open for 0% of the time, Pallas kernels for 0%

profile of v1, /device:TPU:1, one launch (start us, length us, event | category | flops | bytes accessed | tf_op | source)
XLA Modules:
  0.0 110.6 jit_solution(13448114024526816084)
XLA Ops:
  0.6 1.4 %copy.14.pattern_ref = s32[16,4]{1,0:T(8,128)} copy(s32[16,4]{0,1:T(4,128)} %param.9) | data formatting | bytes 512 | tf_op args[3]
  2.6 4.6 %assemble.1 = f32[1088,128]{1,0:T(8,128)} custom-call(s32[1]{0:T(128)S(6)} %copy.18.count_ref, s32[16,4]{1,0:T(8,128)} %copy.14.pattern_ref, bf16[2048,512]{1,0:T(8,128)(2,1)} %rows_hbm.3, f32[16,128]{1,0:T(8,128)} %bitcast.5, f32[16,128]{1,0:T(8,128)} %bitcast.7), custom_call_target="tpu_custom_call" | custom-call | tf_op jit(solution)/shard_map/assemble/pallas_call | solution.py:90
  7.3 1.0 constant_dynamic-slice_fusion
  8.2 8.7 %collective-permute-start = (f32[544,128]{1,0:T(8,128)S(1)}, f32[544,128]{1,0:T(8,128)S(1)}, u32[]{:S(2)}, u32[]{:S(2)}) collective-permute-start(f32[544,128]{1,0:T(8,128)S(1)} %constant_dynamic-slice_fusion), channel_id=1, source_target_pairs={{0,32},{32,0},{1,33},{33,1},{2,34},{34,2},{3,35},{35,3},{4,36},{36... | collective-permute-start | bytes 835592 | tf_op jit(solution)/shard_map/ppermute | solution.py:219
  17.0 1.2 %collective-permute-done = f32[544,128]{1,0:T(8,128)S(1)} collective-permute-done((f32[544,128]{1,0:T(8,128)S(1)}, f32[544,128]{1,0:T(8,128)S(1)}, u32[]{:S(2)}, u32[]{:S(2)}) %collective-permute-start) | collective-permute-done | bytes 278560 | tf_op jit(solution)/shard_map/ppermute | solution.py:219
  18.2 1.0 dynamic-slice_add_fusion
  19.2 18.0 %all_to_all.15 = f32[32,17,128]{2,1,0:T(8,128)S(1)} all-to-all(f32[32,17,128]{2,1,0:T(8,128)S(1)} %reshape.29), channel_id=1, replica_groups=mesh['z'=8,'core'=2,'y'=8,'x'=4] {'y','x'}, dimensions={0} | all-to-all | bytes 557056 | tf_op jit(solution)/shard_map/all_to_all | solution.py:211
  37.2 17.4 %all_to_all.16 = f32[8,17,128]{2,1,0:T(8,128)S(1)} all-to-all(f32[8,17,128]{2,1,0:T(8,128)S(1)} %broadcast_in_dim.4), channel_id=1, replica_groups=mesh['z'=8,'core'=2,'y'=8,'x'=4] {'z'}, dimensions={0} | all-to-all | bytes 139264 | tf_op jit(solution)/shard_map/all_to_all | solution.py:211
  54.7 16.3 %all_to_all.17 = f32[32,17,128]{2,1,0:T(8,128)S(1)} all-to-all(f32[32,17,128]{2,1,0:T(8,128)S(1)} %broadcast_in_dim.5), channel_id=1, replica_groups=mesh['z'=8,'core'=2,'y'=8,'x'=4] {'y','x'}, dimensions={0} | all-to-all | bytes 557056 | tf_op jit(solution)/shard_map/all_to_all | solution.py:211
  71.1 7.4 %collective-permute-start.1 = (f32[544,128]{1,0:T(8,128)S(1)}, f32[544,128]{1,0:T(8,128)S(1)}, u32[]{:S(2)}, u32[]{:S(2)}) collective-permute-start(f32[544,128]{1,0:T(8,128)S(1)} %reshape.30), channel_id=1, source_target_pairs={{0,32},{32,0},{1,33},{33,1},{2,34},{34,2},{3,35},{35,3},{4,36},{36... | collective-permute-start | bytes 835592 | tf_op jit(solution)/shard_map/ppermute | solution.py:225
  78.5 1.0 collective-permute-done.1
  79.5 0.8 maximum_select_fusion.packed_ref
  80.3 30.1 %solve.1 = (f32[16,128]{1,0:T(8,128)}, f32[4,128]{1,0:T(4,128)}) custom-call(s32[1]{0:T(128)S(6)} %copy.18.count_ref, bf16[2048,512]{1,0:T(8,128)(2,1)} %rows_hbm.3, f32[1088,128]{1,0:T(8,128)} %maximum_select_fusion.packed_ref, f32[4,128]{1,0:T(4,128)} %bitcast.9, f32[16,128]{1,0:T(8,128)} %bitcast.6, f32[16,128]{1,0:T(8,128)} %bitcast.8, ...), custom_call_target="tpu_custom_call" | custom-call | tf_op jit(solution)/shard_map/solve/pallas_call | solution.py:195
  (6 shorter events, 0.1 us)
Async XLA Ops:
  8.2 9.9 %collective-permute-start = (f32[544,128]{1,0:T(8,128)S(1)}, f32[544,128]{1,0:T(8,128)S(1)}, u32[]{:S(2)}, u32[]{:S(2)}) collective-permute-start(f32[544,128]{1,0:T(8,128)S(1)} %constant_dynamic-slice_fusion), channel_id=1, source_target_pairs={{0,32},{32,0},{1,33},{33,1},{2,34},{34,2},{3,35},{35,3},{4,36},{36... | collective-permute-start | bytes 835592 | tf_op jit(solution)/shard_map/ppermute | solution.py:219
  71.1 8.4 %collective-permute-start.1 = (f32[544,128]{1,0:T(8,128)S(1)}, f32[544,128]{1,0:T(8,128)S(1)}, u32[]{:S(2)}, u32[]{:S(2)}) collective-permute-start(f32[544,128]{1,0:T(8,128)S(1)} %reshape.30), channel_id=1, source_target_pairs={{0,32},{32,0},{1,33},{33,1},{2,34},{34,2},{3,35},{35,3},{4,36},{36... | collective-permute-start | bytes 835592 | tf_op jit(solution)/shard_map/ppermute | solution.py:225

commit v2 on v1

v2 whole, which is shorter than its diff:
```python
import functools

import jax
import jax.numpy as jnp
from jax import lax
from jax.experimental import pallas as pl
from jax.experimental.pallas import tpu as pltpu
from jax.sharding import Mesh, PartitionSpec as P

TILE = 128
WIDTH = 512
ROWS = 2048
TILES = ROWS // TILE
CHUNKS = 4
F32 = jnp.float32
BF16 = jnp.bfloat16
HIGH = lax.Precision.HIGHEST
HALF = 544
NAMES = ("z", "core", "y", "x")


def iota(shape, axis):
    return lax.broadcasted_iota(jnp.int32, shape, axis)


def dot_nn(a, b):
    return lax.dot_general(a, b, (((1,), (0,)), ((), ())), precision=HIGH, preferred_element_type=F32)


def dot_nt(a, b):
    return lax.dot_general(a, b, (((1,), (1,)), ((), ())), precision=HIGH, preferred_element_type=F32)


def assemble_kernel(
    core_ref, count_ref, pattern_ref, rows_hbm, weights_ref, resid_ref, keep_ref, give_ref, rows, scaled, sems
):
    step = ROWS // CHUNKS
    copies = [
        pltpu.make_async_copy(rows_hbm.at[pl.ds(i * step, step)], rows.at[pl.ds(i * step, step)], sems.at[i])
        for i in range(CHUNKS)
    ]
    for copy in copies:
        copy.start()
    count = count_ref[0]
    shape = (TILES, TILE)
    live = (iota(shape, 0) * TILE + iota(shape, 1) < count).astype(F32)
    weights = weights_ref[...]
    root = jnp.sqrt(weights) * live
    weighted = (weights * resid_ref[...] * live).astype(BF16).astype(F32)
    columns = jnp.concatenate([root, weighted, jnp.zeros((TILE - 2 * TILES, TILE), F32)], axis=0).T
    gradient = [jnp.zeros((8, TILE), F32) for _ in range(4)]
    for t in range(TILES):
        if t % (TILES // CHUNKS) == 0:
            copies[t // (TILES // CHUNKS)].wait()
        root_t = jnp.broadcast_to(columns[:, t : t + 1], (TILE, TILE))
        weighted_t = jnp.broadcast_to(columns[:, TILES + t : TILES + t + 1], (TILE, TILE))
        for j in range(4):
            cover = pattern_ref[j, t].astype(F32)
            x = rows[pl.ds(t * TILE, TILE), pl.ds(j * TILE, TILE)].astype(F32) * cover
            scaled[pl.ds(t * TILE, TILE), pl.ds(j * TILE, TILE)] = (x * root_t).astype(BF16)
            gradient[j] = gradient[j] + jnp.sum((x * weighted_t).reshape(TILE // 8, 8, TILE), axis=0)
    below = iota((TILE, TILE), 0) >= iota((TILE, TILE), 1)
    same = iota((TILE, TILE), 0) == iota((TILE, TILE), 1)

    def gram(i, j):
        return lax.dot_general(
            scaled[:, pl.ds(i * 256, 256)],
            scaled[:, pl.ds(j * 256, 256)],
            (((0,), (0,)), ((), ())),
            preferred_element_type=F32,
        )

    def finish(out_ref, block, corner, pieces, first):
        a, b = block[:TILE, :TILE], block[TILE:, TILE:]
        out_ref[pl.ds(0, TILE), :] = jnp.where(below, a, b)
        out_ref[pl.ds(TILE, TILE), :] = corner
        for i, piece in enumerate(pieces):
            out_ref[pl.ds((2 + i) * TILE, TILE), :] = piece
        diagonal = jnp.sum(jnp.where(same, b, 0.0), axis=0, keepdims=True)
        parts = [jnp.sum(gradient[first], axis=0, keepdims=True), jnp.sum(gradient[first + 1], axis=0, keepdims=True), diagonal]
        out_ref[pl.ds(4 * TILE, 8), :] = jnp.concatenate(parts + [jnp.zeros((5, TILE), F32)], axis=0)
        out_ref[pl.ds(4 * TILE + 8, 24), :] = jnp.zeros((24, TILE), F32)

    top, low, cross = gram(0, 0), gram(1, 1), gram(1, 0)

    def both(first_ref, second_ref):
        finish(first_ref, top, top[TILE:, :TILE], (cross[:TILE, :TILE], cross[TILE:, :TILE]), 0)
        finish(second_ref, low, low[TILE:, :TILE], (cross[:TILE, TILE:], cross[TILE:, TILE:]), 2)

    @pl.when(core_ref[0] == 0)
    def _():
        both(keep_ref, give_ref)

    @pl.when(core_ref[0] != 0)
    def _():
        both(give_ref, keep_ref)


def assemble(core, count, pattern, rows, weights, resid):
    vmem = pl.BlockSpec(memory_space=pltpu.VMEM)
    smem = pl.BlockSpec(memory_space=pltpu.SMEM)
    half = jax.ShapeDtypeStruct((HALF, TILE), F32)
    return pl.pallas_call(
        assemble_kernel,
        out_shape=(half, half),
        in_specs=[smem, smem, smem, pl.BlockSpec(memory_space=pl.ANY), vmem, vmem],
        out_specs=(vmem, vmem),
        scratch_shapes=[
            pltpu.VMEM((ROWS, WIDTH), BF16),
            pltpu.VMEM((ROWS, WIDTH), BF16),
            pltpu.SemaphoreType.DMA((CHUNKS,)),
        ],
        name="assemble",
    )(core, count, pattern, rows, weights, resid)


def wide(v):
    return jnp.broadcast_to(v, (8, TILE))


def eliminate(groups, first):
    lane, sub = iota((8, TILE), 1), iota((8, TILE), 0)
    groups = list(groups)
    for k in range(8):
        start = first + 8 * k
        cols = [wide(groups[k][:, start + j : start + j + 1]) for j in range(8)]
        inside = (lane >= start) & (lane < start + 8)
        panel = jnp.where(inside, (lane - start == sub).astype(F32), groups[k])
        for j in range(8):
            here = sub == j
            inverse = 1.0 / wide(cols[j][j : j + 1, :])
            pivot = cols[j]
            scaled_row = wide(panel[j : j + 1, :]) * inverse
            panel = jnp.where(here, scaled_row, panel - pivot * scaled_row)
            for c in range(j + 1, 8):
                entry = wide(cols[c][j : j + 1, :]) * inverse
                cols[c] = jnp.where(here, entry, cols[c] - pivot * entry)
        spread = [wide(panel[j : j + 1, :]) for j in range(8)]
        order = [(k + 1 + i) % 8 for i in range(7)]
        for i in order:
            terms = [wide(groups[i][:, start + j : start + j + 1]) * spread[j] for j in range(8)]
            total = ((terms[0] + terms[1]) + (terms[2] + terms[3])) + ((terms[4] + terms[5]) + (terms[6] + terms[7]))
            groups[i] = jnp.where(inside, 0.0, groups[i]) - total
        groups[k] = panel
    return groups


def invert(block):
    half = TILE // 2
    lane = iota((half, TILE), 1)
    zeros = jnp.zeros((half, TILE), F32)
    top, low = block[:half], block[half:]
    split = lambda v: [v[8 * i : 8 * i + 8] for i in range(8)]
    top = jnp.concatenate(eliminate(split(top), 0), axis=0)
    low = jnp.where(lane < half, 0.0, low) - dot_nn(low, jnp.concatenate([top, zeros], axis=0))
    low = jnp.concatenate(eliminate(split(low), half), axis=0)
    top = jnp.where(lane < half, top, 0.0) - dot_nn(top, jnp.concatenate([zeros, low], axis=0))
    return jnp.concatenate([top, low], axis=0)


def solve_kernel(
    core_ref, count_ref, pattern_ref, rows_hbm, mine_ref, other_ref, diag_ref, weights_ref, resid_ref,
    row_step_ref, step_ref, rows, matrix, inverses, sem,
):
    copy = pltpu.make_async_copy(rows_hbm, rows, sem)
    copy.start()
    below = iota((TILE, TILE), 0) >= iota((TILE, TILE), 1)
    same = iota((TILE, TILE), 0) == iota((TILE, TILE), 1)
    link = diag_ref[...]
    core = core_ref[0]

    def tile(i, j):
        return pl.ds(i * TILE, TILE), pl.ds(j * TILE, TILE)

    gradient = []
    for h in range(2):

        def part(start, size):
            return jnp.where(core == h, mine_ref[pl.ds(start, size), :], other_ref[pl.ds(start, size), :])

        folded = part(0, TILE)
        turned = folded.T
        extras = part(4 * TILE, 8)
        gradient += [extras[0:1], extras[1:2]]
        i = 2 * h
        matrix[tile(i, i)] = jnp.where(below, folded, turned) + jnp.where(same, link[i : i + 1, :], 0.0)
        matrix[tile(i + 1, i + 1)] = jnp.where(same, extras[2:3] + link[i + 1 : i + 2, :], jnp.where(below, turned, folded))
        matrix[tile(i + 1, i)] = part(TILE, TILE)
        matrix[tile(2, h)] = part(2 * TILE, TILE)
        matrix[tile(3, h)] = part(3 * TILE, TILE)
    factors = {}
    for k in range(4):
        inverse = invert(matrix[tile(k, k)])
        inverses[k] = inverse
        for i in range(k + 1, 4):
            factors[i, k] = dot_nn(matrix[tile(i, k)], inverse)
        for i in range(k + 1, 4):
            gradient[i] = gradient[i] - dot_nt(gradient[k], factors[i, k])
            for j in range(k + 1, i + 1):
                matrix[tile(i, j)] = matrix[tile(i, j)] - dot_nt(factors[i, k], matrix[tile(j, k)])
    steps = [None] * 4
    for k in reversed(range(4)):
        value = dot_nn(gradient[k], inverses[k])
        for i in range(k + 1, 4):
            value = value - dot_nn(steps[i], factors[i, k])
        steps[k] = value
    step_ref[...] = jnp.concatenate(steps, axis=0)
    copy.wait()
    shape = (TILES, TILE)
    left = []
    for j in range(4):
        present = jnp.zeros(shape, F32)
        for t in range(TILES):
            present = jnp.where(iota(shape, 0) == t, pattern_ref[j, t].astype(F32), present)
        left.append(jnp.broadcast_to(steps[j], shape) * present)
    left = jnp.concatenate(left, axis=1).astype(BF16)
    moved = jnp.zeros(shape, F32)
    for t in range(TILES):
        part = lax.dot_general(
            left, rows[pl.ds(t * TILE, TILE), :], (((1,), (1,)), ((), ())), preferred_element_type=F32
        )
        moved = jnp.where(iota(shape, 0) == t, part, moved)
    live = (iota(shape, 0) * TILE + iota(shape, 1) < count_ref[0]).astype(F32)
    row_step_ref[...] = live * weights_ref[...] * (moved - resid_ref[...])


def solve(core, count, pattern, rows, mine, other, diag, weights, resid):
    vmem = pl.BlockSpec(memory_space=pltpu.VMEM)
    smem = pl.BlockSpec(memory_space=pltpu.SMEM)
    return pl.pallas_call(
        solve_kernel,
        out_shape=(jax.ShapeDtypeStruct((TILES, TILE), F32), jax.ShapeDtypeStruct((4, TILE), F32)),
        in_specs=[smem, smem, smem, pl.BlockSpec(memory_space=pl.ANY)] + [vmem] * 5,
        out_specs=(vmem, vmem),
        scratch_shapes=[
            pltpu.VMEM((ROWS, WIDTH), BF16),
            pltpu.VMEM((WIDTH, WIDTH), F32),
            pltpu.VMEM((4, TILE, TILE), F32),
            pltpu.SemaphoreType.DMA,
        ],
        name="solve",
    )(core, count, pattern, rows, mine, other, diag, weights, resid)


def exchange(x, axes):
    return lax.all_to_all(x, axes, split_axis=0, concat_axis=0, tiled=True)


def reduce_all(keep, give):
    swap = [(0, 1), (1, 0)]
    half = keep + lax.ppermute(give, "core", swap)
    pieces = exchange(half.reshape(32, 17, TILE), ("y", "x"))
    piece = jnp.sum(pieces, axis=0)
    layers = exchange(jnp.broadcast_to(piece[None], (8, 17, TILE)), "z")
    piece = jnp.sum(layers, axis=0)
    half = exchange(jnp.broadcast_to(piece[None], (32, 17, TILE)), ("y", "x")).reshape(HALF, TILE)
    return half, lax.ppermute(half, "core", swap)


def on_device(link_rows, barrier_weights, row_residual, tile_pattern, block_rows, link_diag):
    weights = barrier_weights.reshape(TILES, TILE)
    resid = row_residual.reshape(TILES, TILE)
    core = lax.axis_index("core").astype(jnp.int32).reshape(1)
    pattern = tile_pattern.T
    mine, other = reduce_all(*assemble(core, block_rows, pattern, link_rows, weights, resid))
    row_step, step = solve(core, block_rows, pattern, link_rows, mine, other, link_diag.reshape(4, TILE), weights, resid)
    return row_step.reshape(ROWS), step.reshape(WIDTH)


def solution(mesh):
    fine = Mesh(mesh.devices.reshape(8, 2, 8, 4), NAMES)
    return jax.shard_map(
        on_device,
        mesh=fine,
        in_specs=(P(NAMES, None), P(NAMES), P(NAMES), P(NAMES, None), P(NAMES), P()),
        out_specs=(P(NAMES), P()),
        check_vma=False,
    )
```

time: 111 us -> 104 us (0.937)
  Pallas kernels: 34.8 us -> 30 us
  local copies, waits for them, and re-layouts: 2.42 us -> 0.8 us
    pallas_call x1, Pallas kernels: 30.1 us -> 25.4 us  [solve(): pl.pallas_call(solve_kernel, out_shape=(jax.ShapeDtypeStruct((TILES, TILE...]
where the time goes in v2:
time: 104 us
  blocking collectives  51.7 us (50%)
  Pallas kernels  30 us (29%)
  starting transfers between devices  16.1 us (15%)
  waiting for transfers between devices  2.36 us (2%)
  between operations  1.51 us (1%)
  other arithmetic  1.05 us (1%)
    all_to_all x3, blocking collectives, exchange(): return lax.all_to_all(x, axes, split_axis=0, concat_axis=0, tiled=True)  51.7 us
    pallas_call x1, Pallas kernels, solve(): pl.pallas_call(solve_kernel, out_shape=(jax.ShapeDtypeStruct((TILES, TILE...  25.4 us
    ppermute x1, starting transfers between devices, reduce_all(): half = keep + lax.ppermute(give, 'core', swap)  8.73 us
    ppermute x1, starting transfers between devices, reduce_all(): return (half, lax.ppermute(half, 'core', swap))  7.38 us
    pallas_call x1, Pallas kernels, assemble(): pl.pallas_call(assemble_kernel, out_shape=(half, half), in_specs=[smem, s...  4.62 us
  transfers between devices with their start and end apart: 2, of which 2 were waited for; matrix products, arithmetic and copies ran while one was open for 0% of the time, Pallas kernels for 0%

profile of v2, /device:TPU:1, one launch (start us, length us, event | category | flops | bytes accessed | tf_op | source)
XLA Modules:
  0.0 103.6 jit_solution(14278745278924060648)
XLA Ops:
  1.3 4.6 %assemble.1 = (f32[544,128]{1,0:T(8,128)}, f32[544,128]{1,0:T(8,128)}) custom-call(s32[1]{0:T(128)} %bitcast.core_ref, s32[1]{0:T(128)S(6)} %copy.10.count_ref, s32[4,16]{1,0:T(4,128)} %bitcast.11, bf16[2048,512]{1,0:T(8,128)(2,1)} %rows_hbm.3, f32[16,128]{1,0:T(8,128)} %bitcast.7, f32[16,128]{1,0:T(8,128)} %bitcast.9), custom_call_target="tpu_custom_call" | custom-call | tf_op jit(solution)/shard_map/assemble/pallas_call | solution.py:103
  5.9 8.7 %collective-permute-start = (f32[544,128]{1,0:T(8,128)}, f32[544,128]{1,0:T(8,128)S(1)}, u32[]{:S(2)}, u32[]{:S(2)}) collective-permute-start(f32[544,128]{1,0:T(8,128)} %get-tuple-element.7), channel_id=1, source_target_pairs={{0,32},{32,0},{1,33},{33,1},{2,34},{34,2},{3,35},{35,3},{4,36},{36... | collective-permute-start | bytes 835592 | tf_op jit(solution)/shard_map/ppermute | solution.py:251
  14.6 1.4 %collective-permute-done = f32[544,128]{1,0:T(8,128)S(1)} collective-permute-done((f32[544,128]{1,0:T(8,128)}, f32[544,128]{1,0:T(8,128)S(1)}, u32[]{:S(2)}, u32[]{:S(2)}) %collective-permute-start) | collective-permute-done | bytes 278560 | tf_op jit(solution)/shard_map/ppermute | solution.py:251
  16.0 1.0 add.3
  17.1 18.0 %all_to_all.15 = f32[32,17,128]{2,1,0:T(8,128)S(1)} all-to-all(f32[32,17,128]{2,1,0:T(8,128)S(1)} %reshape.33), channel_id=1, replica_groups=mesh['z'=8,'core'=2,'y'=8,'x'=4] {'y','x'}, dimensions={0} | all-to-all | bytes 557056 | tf_op jit(solution)/shard_map/all_to_all | solution.py:246
  35.1 17.4 %all_to_all.16 = f32[8,17,128]{2,1,0:T(8,128)S(1)} all-to-all(f32[8,17,128]{2,1,0:T(8,128)S(1)} %broadcast_in_dim.4), channel_id=1, replica_groups=mesh['z'=8,'core'=2,'y'=8,'x'=4] {'z'}, dimensions={0} | all-to-all | bytes 139264 | tf_op jit(solution)/shard_map/all_to_all | solution.py:246
  52.6 16.3 %all_to_all.17 = f32[32,17,128]{2,1,0:T(8,128)S(1)} all-to-all(f32[32,17,128]{2,1,0:T(8,128)S(1)} %broadcast_in_dim.5), channel_id=1, replica_groups=mesh['z'=8,'core'=2,'y'=8,'x'=4] {'y','x'}, dimensions={0} | all-to-all | bytes 557056 | tf_op jit(solution)/shard_map/all_to_all | solution.py:246
  68.9 0.0 copy-start
  69.0 7.4 %collective-permute-start.1 = (f32[544,128]{1,0:T(8,128)S(1)}, f32[544,128]{1,0:T(8,128)S(1)}, u32[]{:S(2)}, u32[]{:S(2)}) collective-permute-start(f32[544,128]{1,0:T(8,128)S(1)} %reshape.34.mine_ref), channel_id=1, source_target_pairs={{0,32},{32,0},{1,33},{33,1},{2,34},{34,2},{3,35},{35,3},{4,36},{36... | collective-permute-start | bytes 835592 | tf_op jit(solution)/shard_map/ppermute | solution.py:257
  76.3 1.0 collective-permute-done.1.other_ref
  77.3 0.0 copy-start.1
  77.3 0.0 copy-done
  77.3 0.7 copy-done.1
  78.0 25.4 %solve.1 = (f32[16,128]{1,0:T(8,128)}, f32[4,128]{1,0:T(4,128)}) custom-call(s32[1]{0:T(128)} %bitcast.core_ref, s32[1]{0:T(128)S(6)} %copy.10.count_ref, s32[4,16]{1,0:T(4,128)} %bitcast.12, bf16[2048,512]{1,0:T(8,128)(2,1)} %rows_hbm.3, f32[544,128]{1,0:T(8,128)} %copy-done, f32[544,128]{1,0:T(8,128)} %copy-done.1, f32[4,128]{1,0:T(4,128)} %bitcast.13, ...), custom_call_target="tpu_custom_call" | custom-call | tf_op jit(solution)/shard_map/solve/pallas_call | solution.py:230
  (6 shorter events, 0.1 us)
Async XLA Ops:
  5.9 10.1 %collective-permute-start = (f32[544,128]{1,0:T(8,128)}, f32[544,128]{1,0:T(8,128)S(1)}, u32[]{:S(2)}, u32[]{:S(2)}) collective-permute-start(f32[544,128]{1,0:T(8,128)} %get-tuple-element.7), channel_id=1, source_target_pairs={{0,32},{32,0},{1,33},{33,1},{2,34},{34,2},{3,35},{35,3},{4,36},{36... | collective-permute-start | bytes 835592 | tf_op jit(solution)/shard_map/ppermute | solution.py:251
  68.9 8.4 %copy-start = (f32[544,128]{1,0:T(8,128)}, f32[544,128]{1,0:T(8,128)S(1)}, u32[]{:S(2)}) copy-start(f32[544,128]{1,0:T(8,128)S(1)} %reshape.34.mine_ref) | copy-start | bytes 835588
  69.0 8.4 %collective-permute-start.1 = (f32[544,128]{1,0:T(8,128)S(1)}, f32[544,128]{1,0:T(8,128)S(1)}, u32[]{:S(2)}, u32[]{:S(2)}) collective-permute-start(f32[544,128]{1,0:T(8,128)S(1)} %reshape.34.mine_ref), channel_id=1, source_target_pairs={{0,32},{32,0},{1,33},{33,1},{2,34},{34,2},{3,35},{35,3},{4,36},{36... | collective-permute-start | bytes 835592 | tf_op jit(solution)/shard_map/ppermute | solution.py:257
  77.3 0.7 copy-start.1

commit v3 on v2

--- a/solution.py
+++ b/solution.py
@@ -118,49 +118,95 @@
     return jnp.broadcast_to(v, (8, TILE))
 
 
-def eliminate(groups, first):
+def spread_lane(v, lane):
+    return jnp.take_along_axis(v, jnp.full((8, TILE), lane, jnp.int32), axis=1)
+
+
+def eliminate(rows, first, once, tasks):
     lane, sub = iota((8, TILE), 1), iota((8, TILE), 0)
-    groups = list(groups)
+    groups = [rows[8 * k : 8 * k + 8] for k in range(8)]
+    sides = [(lane - first - 8 * k == sub).astype(F32) for k in range(8)]
+    lower, scaled = [], []
     for k in range(8):
         start = first + 8 * k
-        cols = [wide(groups[k][:, start + j : start + j + 1]) for j in range(8)]
-        inside = (lane >= start) & (lane < start + 8)
-        panel = jnp.where(inside, (lane - start == sub).astype(F32), groups[k])
-        for j in range(8):
-            here = sub == j
-            inverse = 1.0 / wide(cols[j][j : j + 1, :])
-            pivot = cols[j]
-            scaled_row = wide(panel[j : j + 1, :]) * inverse
-            panel = jnp.where(here, scaled_row, panel - pivot * scaled_row)
-            for c in range(j + 1, 8):
-                entry = wide(cols[c][j : j + 1, :]) * inverse
-                cols[c] = jnp.where(here, entry, cols[c] - pivot * entry)
-        spread = [wide(panel[j : j + 1, :]) for j in range(8)]
-        order = [(k + 1 + i) % 8 for i in range(7)]
-        for i in order:
-            terms = [wide(groups[i][:, start + j : start + j + 1]) * spread[j] for j in range(8)]
-            total = ((terms[0] + terms[1]) + (terms[2] + terms[3])) + ((terms[4] + terms[5]) + (terms[6] + terms[7]))
-            groups[i] = jnp.where(inside, 0.0, groups[i]) - total
-        groups[k] = panel
-    return groups
-
-
-def invert(block):
+
+        todo = tasks.pop(0) if tasks and k >= tasks[0][0] else None
+
+        def body(_, carry):
+            if todo:
+                todo[1]()
+            groups, sides = list(carry[: 8 - k]), list(carry[8 - k :])
+            cols = [spread_lane(groups[0], start + j) for j in range(8)]
+            panel, side = groups[0], sides[0]
+            for j in range(8):
+                here = sub == j
+                pivot = cols[j]
+                inverse = 1.0 / wide(pivot[j : j + 1, :])
+                row, side_row = wide(panel[j : j + 1, :]) * inverse, wide(side[j : j + 1, :]) * inverse
+                for c in range(j + 1, 8):
+                    entry = wide(cols[c][j : j + 1, :]) * inverse
+                    cols[c] = jnp.where(here, entry, cols[c] - pivot * entry)
+                panel = jnp.where(here, row, panel - pivot * row)
+                side = jnp.where(here, side_row, side - pivot * side_row)
+            spread = [wide(panel[j : j + 1, :]) for j in range(8)]
+            spread_side = [wide(side[j : j + 1, :]) for j in range(8)]
+            for i in range(1, 8 - k):
+                lead = [spread_lane(groups[i], start + j) for j in range(8)]
+                groups[i] = groups[i] - add_up([lead[j] * spread[j] for j in range(8)])
+                sides[i] = sides[i] - add_up([lead[j] * spread_side[j] for j in range(8)])
+            return (*groups[1:], panel, *sides[1:], side)
+
+        lower.append(sides[0])
+        carry = lax.fori_loop(0, once, body, (*groups, *sides))
+        groups, sides = list(carry[: 7 - k]), list(carry[8 - k : -1])
+        scaled.append(carry[-1])
+    return jnp.concatenate(lower, axis=0), jnp.concatenate(scaled, axis=0)
+
+
+def add_up(terms):
+    while len(terms) > 1:
+        terms = [terms[i] + terms[i + 1] for i in range(0, len(terms), 2)]
+    return terms[0]
+
+
+def thirds(x):
+    high = x.astype(BF16)
+    rest = x - high.astype(F32)
+    middle = rest.astype(BF16)
+    return high, middle, (rest - middle.astype(F32)).astype(BF16)
+
+
+def as_left(x):
+    h, m, l = thirds(x)
+    return jnp.concatenate([h, m, h, m, h, l], axis=1)
+
+
+def as_right(x, axis=1):
+    h, m, l = thirds(x)
+    return jnp.concatenate([h, h, m, m, l, h], axis=axis)
+
+
+def times(left, right, dim=1):
+    return lax.dot_general(left, right, (((1,), (dim,)), ((), ())), preferred_element_type=F32)
+
+
+def factor(block, once, cross, tasks):
     half = TILE // 2
-    lane = iota((half, TILE), 1)
     zeros = jnp.zeros((half, TILE), F32)
-    top, low = block[:half], block[half:]
-    split = lambda v: [v[8 * i : 8 * i + 8] for i in range(8)]
-    top = jnp.concatenate(eliminate(split(top), 0), axis=0)
-    low = jnp.where(lane < half, 0.0, low) - dot_nn(low, jnp.concatenate([top, zeros], axis=0))
-    low = jnp.concatenate(eliminate(split(low), half), axis=0)
-    top = jnp.where(lane < half, top, 0.0) - dot_nn(top, jnp.concatenate([zeros, low], axis=0))
-    return jnp.concatenate([top, low], axis=0)
+    low = block[half:]
+    lower, scaled = eliminate(block[:half], 0, once, tasks)
+    pair = times(as_left(low), as_right(jnp.concatenate([lower, zeros, scaled, zeros], axis=0)))
+    left = as_left(pair[:, :TILE])
+    low = low - times(left, as_right(jnp.concatenate([zeros, pair[:, TILE:]], axis=0)))
+    cross[pl.ds(half, half), :] = times(left, as_right(jnp.concatenate([scaled, zeros], axis=0), 0), 0)
+    both = jnp.concatenate(eliminate(low, half, once, tasks), axis=0)
+    both = both - times(as_left(both), as_right(cross[...], 0), 0)
+    return jnp.concatenate([lower, both[:half]], axis=0), jnp.concatenate([scaled, both[half:]], axis=0)
 
 
 def solve_kernel(
     core_ref, count_ref, pattern_ref, rows_hbm, mine_ref, other_ref, diag_ref, weights_ref, resid_ref,
-    row_step_ref, step_ref, rows, matrix, inverses, sem,
+    row_step_ref, step_ref, rows, matrix, lefts, left_parts, right_parts, both_parts, scales, cross, sem,
 ):
     copy = pltpu.make_async_copy(rows_hbm, rows, sem)
     copy.start()
@@ -188,22 +234,46 @@
         matrix[tile(i + 1, i)] = part(TILE, TILE)
         matrix[tile(2, h)] = part(2 * TILE, TILE)
         matrix[tile(3, h)] = part(3 * TILE, TILE)
-    factors = {}
-    for k in range(4):
-        inverse = invert(matrix[tile(k, k)])
-        inverses[k] = inverse
-        for i in range(k + 1, 4):
-            factors[i, k] = dot_nn(matrix[tile(i, k)], inverse)
-        for i in range(k + 1, 4):
-            gradient[i] = gradient[i] - dot_nt(gradient[k], factors[i, k])
-            for j in range(k + 1, i + 1):
-                matrix[tile(i, j)] = matrix[tile(i, j)] - dot_nt(factors[i, k], matrix[tile(j, k)])
+    once = jnp.minimum(count_ref[0], 1)
+    cross[...] = jnp.zeros((TILE, TILE), F32)
+    matrix[pl.ds(WIDTH, 16), :] = jnp.broadcast_to(jnp.concatenate(gradient, axis=1), (16, WIDTH))
+
+    def span(i):
+        return pl.ds(i * TILE, TILE if i < 3 else TILE + 16)
+
+    def project(i, q, both):
+        pair = times(as_left(matrix[span(i), pl.ds(q * TILE, TILE)]), both)
+        lefts[q, span(i), :] = pair[:, :TILE]
+        left_parts[span(i), :] = as_left(pair[:, :TILE])
+        right_parts[pl.ds(i * TILE, TILE), :] = as_right(pair[:TILE, TILE:])
+
+    def update(i, j, count):
+        columns = pl.ds(j * TILE, count * TILE)
+        matrix[span(i), columns] -= times(left_parts[span(i), :], right_parts[columns, :])
+
+    tasks = []
+    for q in range(4):
+        lower, scaled = factor(matrix[tile(q, q)], once, cross, tasks)
+        assert not tasks
+        scales[q] = scaled
+        both_parts[...] = as_right(jnp.concatenate([lower, scaled], axis=0))
+        if q == 3:
+            break
+        project(q + 1, q, both_parts[...])
+        update(q + 1, q + 1, 1)
+        for i in range(q + 2, 4):
+            tasks.append((1, functools.partial(lambda i, q: project(i, q, both_parts[...]), i, q)))
+        for i in range(q + 2, 4):
+            tasks.append((1, functools.partial(update, i, q + 1, 2)))
+            if i == q + 3:
+                tasks.append((1, functools.partial(update, i, i, 1)))
+    last = times(as_left(matrix[pl.ds(WIDTH, 16), pl.ds(3 * TILE, TILE)]), both_parts[pl.ds(0, TILE), :])
     steps = [None] * 4
-    for k in reversed(range(4)):
-        value = dot_nn(gradient[k], inverses[k])
-        for i in range(k + 1, 4):
-            value = value - dot_nn(steps[i], factors[i, k])
-        steps[k] = value
+    for q in reversed(range(4)):
+        value = last[:1] if q == 3 else lefts[q, pl.ds(WIDTH, 8), :][:1]
+        for i in range(q + 1, 4):
+            value = value - dot_nn(steps[i], lefts[q, pl.ds(i * TILE, TILE), :])
+        steps[q] = dot_nn(value, scales[q])
     step_ref[...] = jnp.concatenate(steps, axis=0)
     copy.wait()
     shape = (TILES, TILE)
@@ -234,8 +304,13 @@
         out_specs=(vmem, vmem),
         scratch_shapes=[
             pltpu.VMEM((ROWS, WIDTH), BF16),
-            pltpu.VMEM((WIDTH, WIDTH), F32),
+            pltpu.VMEM((WIDTH + 16, WIDTH), F32),
+            pltpu.VMEM((3, WIDTH + 16, TILE), F32),
+            pltpu.VMEM((WIDTH + 16, 6 * TILE), BF16),
+            pltpu.VMEM((WIDTH, 6 * TILE), BF16),
+            pltpu.VMEM((2 * TILE, 6 * TILE), BF16),
             pltpu.VMEM((4, TILE, TILE), F32),
+            pltpu.VMEM((TILE, TILE), F32),
             pltpu.SemaphoreType.DMA,
         ],
         name="solve",

time: 104 us -> 99.5 us (0.957)
  Pallas kernels: 30 us -> 25.7 us
    pallas_call x1, Pallas kernels: 25.4 us -> 21.1 us  [solve(): pl.pallas_call(solve_kernel, out_shape=(jax.ShapeDtypeStruct((TILES, TILE...]
where the time goes in v3:
time: 99.5 us; the launch traced here: 99.1 us
  blocking collectives  51.7 us (52%)
  Pallas kernels  25.7 us (26%)
  starting transfers between devices  15.9 us (16%)
  waiting for transfers between devices  2.54 us (3%)
  between operations  1.35 us (1%)
  other arithmetic  1.05 us (1%)
    all_to_all x3, blocking collectives, exchange(): return lax.all_to_all(x, axes, split_axis=0, concat_axis=0, tiled=True)  51.7 us
    pallas_call x1, Pallas kernels, solve(): pl.pallas_call(solve_kernel, out_shape=(jax.ShapeDtypeStruct((TILES, TILE...  21.1 us
    ppermute x1, starting transfers between devices, reduce_all(): half = keep + lax.ppermute(give, 'core', swap)  8.73 us
    ppermute x1, starting transfers between devices, reduce_all(): return (half, lax.ppermute(half, 'core', swap))  7.2 us
    pallas_call x1, Pallas kernels, assemble(): pl.pallas_call(assemble_kernel, out_shape=(half, half), in_specs=[smem, s...  4.62 us
  transfers between devices with their start and end apart: 2, of which 2 were waited for; matrix products, arithmetic and copies ran while one was open for 0% of the time, Pallas kernels for 0%

profile of v3, /device:TPU:1, one launch (start us, length us, event | category | flops | bytes accessed | tf_op | source)
XLA Modules:
  0.0 99.1 jit_solution(1023297001764719948)
XLA Ops:
  1.3 4.6 %assemble.1 = (f32[544,128]{1,0:T(8,128)}, f32[544,128]{1,0:T(8,128)}) custom-call(s32[1]{0:T(128)} %bitcast.core_ref, s32[1]{0:T(128)S(6)} %copy.10.count_ref, s32[4,16]{1,0:T(4,128)} %bitcast.11, bf16[2048,512]{1,0:T(8,128)(2,1)} %rows_hbm.3, f32[16,128]{1,0:T(8,128)} %bitcast.7, f32[16,128]{1,0:T(8,128)} %bitcast.9), custom_call_target="tpu_custom_call" | custom-call | tf_op jit(solution)/shard_map/assemble/pallas_call | solution.py:103
  5.9 8.7 %collective-permute-start = (f32[544,128]{1,0:T(8,128)}, f32[544,128]{1,0:T(8,128)S(1)}, u32[]{:S(2)}, u32[]{:S(2)}) collective-permute-start(f32[544,128]{1,0:T(8,128)} %get-tuple-element.7), channel_id=1, source_target_pairs={{0,32},{32,0},{1,33},{33,1},{2,34},{34,2},{3,35},{35,3},{4,36},{36... | collective-permute-start | bytes 835592 | tf_op jit(solution)/shard_map/ppermute | solution.py:326
  14.7 1.4 %collective-permute-done = f32[544,128]{1,0:T(8,128)S(1)} collective-permute-done((f32[544,128]{1,0:T(8,128)}, f32[544,128]{1,0:T(8,128)S(1)}, u32[]{:S(2)}, u32[]{:S(2)}) %collective-permute-start) | collective-permute-done | bytes 278560 | tf_op jit(solution)/shard_map/ppermute | solution.py:326
  16.0 1.0 %add.3 = f32[544,128]{1,0:T(8,128)S(1)} add(f32[544,128]{1,0:T(8,128)} %get-tuple-element.6, f32[544,128]{1,0:T(8,128)S(1)} %collective-permute-done) | non-fusion elementwise | flops 69632 | bytes 835584 | tf_op jit(solution)/shard_map/add | solution.py:326
  17.1 18.0 %all_to_all.15 = f32[32,17,128]{2,1,0:T(8,128)S(1)} all-to-all(f32[32,17,128]{2,1,0:T(8,128)S(1)} %reshape.33), channel_id=1, replica_groups=mesh['z'=8,'core'=2,'y'=8,'x'=4] {'y','x'}, dimensions={0} | all-to-all | bytes 557056 | tf_op jit(solution)/shard_map/all_to_all | solution.py:321
  35.1 17.4 %all_to_all.16 = f32[8,17,128]{2,1,0:T(8,128)S(1)} all-to-all(f32[8,17,128]{2,1,0:T(8,128)S(1)} %broadcast_in_dim.4), channel_id=1, replica_groups=mesh['z'=8,'core'=2,'y'=8,'x'=4] {'z'}, dimensions={0} | all-to-all | bytes 139264 | tf_op jit(solution)/shard_map/all_to_all | solution.py:321
  52.6 16.3 %all_to_all.17 = f32[32,17,128]{2,1,0:T(8,128)S(1)} all-to-all(f32[32,17,128]{2,1,0:T(8,128)S(1)} %broadcast_in_dim.5), channel_id=1, replica_groups=mesh['z'=8,'core'=2,'y'=8,'x'=4] {'y','x'}, dimensions={0} | all-to-all | bytes 557056 | tf_op jit(solution)/shard_map/all_to_all | solution.py:321
  68.9 0.0 copy-start
  69.0 7.2 %collective-permute-start.1 = (f32[544,128]{1,0:T(8,128)S(1)}, f32[544,128]{1,0:T(8,128)S(1)}, u32[]{:S(2)}, u32[]{:S(2)}) collective-permute-start(f32[544,128]{1,0:T(8,128)S(1)} %reshape.34.mine_ref), channel_id=1, source_target_pairs={{0,32},{32,0},{1,33},{33,1},{2,34},{34,2},{3,35},{35,3},{4,36},{36... | collective-permute-start | bytes 835592 | tf_op jit(solution)/shard_map/ppermute | solution.py:332
  76.2 1.2 %collective-permute-done.1.other_ref = f32[544,128]{1,0:T(8,128)S(1)} collective-permute-done((f32[544,128]{1,0:T(8,128)S(1)}, f32[544,128]{1,0:T(8,128)S(1)}, u32[]{:S(2)}, u32[]{:S(2)}) %collective-permute-start.1) | collective-permute-done | bytes 278560 | tf_op jit(solution)/shard_map/ppermute | solution.py:332
  77.3 0.0 copy-start.1
  77.3 0.0 copy-done
  77.3 0.7 copy-done.1
  78.0 21.1 %solve.1 = (f32[16,128]{1,0:T(8,128)}, f32[4,128]{1,0:T(4,128)}) custom-call(s32[1]{0:T(128)} %bitcast.core_ref, s32[1]{0:T(128)S(6)} %copy.10.count_ref, s32[4,16]{1,0:T(4,128)} %bitcast.12, bf16[2048,512]{1,0:T(8,128)(2,1)} %rows_hbm.3, f32[544,128]{1,0:T(8,128)} %copy-done, f32[544,128]{1,0:T(8,128)} %copy-done.1, f32[4,128]{1,0:T(4,128)} %bitcast.13, ...), custom_call_target="tpu_custom_call" | custom-call | tf_op jit(solution)/shard_map/solve/pallas_call | solution.py:300
  (6 shorter events, 0.1 us)
Async XLA Ops:
  5.9 10.1 %collective-permute-start = (f32[544,128]{1,0:T(8,128)}, f32[544,128]{1,0:T(8,128)S(1)}, u32[]{:S(2)}, u32[]{:S(2)}) collective-permute-start(f32[544,128]{1,0:T(8,128)} %get-tuple-element.7), channel_id=1, source_target_pairs={{0,32},{32,0},{1,33},{33,1},{2,34},{34,2},{3,35},{35,3},{4,36},{36... | collective-permute-start | bytes 835592 | tf_op jit(solution)/shard_map/ppermute | solution.py:326
  68.9 8.4 %copy-start = (f32[544,128]{1,0:T(8,128)}, f32[544,128]{1,0:T(8,128)S(1)}, u32[]{:S(2)}) copy-start(f32[544,128]{1,0:T(8,128)S(1)} %reshape.34.mine_ref) | copy-start | bytes 835588
  69.0 8.4 %collective-permute-start.1 = (f32[544,128]{1,0:T(8,128)S(1)}, f32[544,128]{1,0:T(8,128)S(1)}, u32[]{:S(2)}, u32[]{:S(2)}) collective-permute-start(f32[544,128]{1,0:T(8,128)S(1)} %reshape.34.mine_ref), channel_id=1, source_target_pairs={{0,32},{32,0},{1,33},{33,1},{2,34},{34,2},{3,35},{35,3},{4,36},{36... | collective-permute-start | bytes 835592 | tf_op jit(solution)/shard_map/ppermute | solution.py:332
  77.3 0.7 copy-start.1

commit v4 on v3

--- a/solution.py
+++ b/solution.py
@@ -99,7 +99,7 @@
 def assemble(core, count, pattern, rows, weights, resid):
     vmem = pl.BlockSpec(memory_space=pltpu.VMEM)
     smem = pl.BlockSpec(memory_space=pltpu.SMEM)
-    half = jax.ShapeDtypeStruct((HALF, TILE), F32)
+    half = pltpu.VMEM((HALF, TILE), F32)
     return pl.pallas_call(
         assemble_kernel,
         out_shape=(half, half),
@@ -338,6 +338,8 @@
     core = lax.axis_index("core").astype(jnp.int32).reshape(1)
     pattern = tile_pattern.T
     mine, other = reduce_all(*assemble(core, block_rows, pattern, link_rows, weights, resid))
+    mine = pltpu.with_memory_space_constraint(mine, pltpu.VMEM)
+    other = pltpu.with_memory_space_constraint(other, pltpu.VMEM)
     row_step, step = solve(core, block_rows, pattern, link_rows, mine, other, link_diag.reshape(4, TILE), weights, resid)
     return row_step.reshape(ROWS), step.reshape(WIDTH)
 

time: 99.5 us -> 96.6 us (0.971)
  Pallas kernels: 25.7 us -> 24.6 us
where the time goes in v4:
time: 96.6 us; the launch traced here: 96.2 us
  blocking collectives  51.8 us (54%)
  Pallas kernels  24.6 us (25%)
  starting transfers between devices  15.9 us (16%)
  waiting for transfers between devices  2.33 us (2%)
  between operations  1.34 us (1%)
    all_to_all x3, blocking collectives, exchange(): return lax.all_to_all(x, axes, split_axis=0, concat_axis=0, tiled=True)  51.8 us
    pallas_call x1, Pallas kernels, solve(): pl.pallas_call(solve_kernel, out_shape=(jax.ShapeDtypeStruct((TILES, TILE...  20.8 us
    ppermute x1, starting transfers between devices, reduce_all(): half = keep + lax.ppermute(give, 'core', swap)  8.73 us
    ppermute x1, starting transfers between devices, reduce_all(): return (half, lax.ppermute(half, 'core', swap))  7.2 us
    pallas_call x1, Pallas kernels, assemble(): pl.pallas_call(assemble_kernel, out_shape=(half, half), in_specs=[smem, s...  3.81 us
  transfers between devices with their start and end apart: 2, of which 2 were waited for; matrix products, arithmetic and copies ran while one was open for 0% of the time, Pallas kernels for 0%

profile of v4, /device:TPU:1, one launch (start us, length us, event | category | flops | bytes accessed | tf_op | source)
XLA Modules:
  0.0 96.2 jit_solution(11317770711211352537)
XLA Ops:
  1.3 3.8 %assemble.1 = (f32[544,128]{1,0:T(8,128)S(1)}, f32[544,128]{1,0:T(8,128)S(1)}) custom-call(s32[1]{0:T(128)} %bitcast.core_ref, s32[1]{0:T(128)S(6)} %copy.10.count_ref, s32[4,16]{1,0:T(4,128)} %bitcast.11, bf16[2048,512]{1,0:T(8,128)(2,1)} %rows_hbm.3, f32[16,128]{1,0:T(8,128)} %bitcast.7, f32[16,128]{1,0:T(8,128)} %bitcast.9), custom_call_target="tpu_custom_call" | custom-call | tf_op jit(solution)/shard_map/assemble/pallas_call | solution.py:103
  5.1 8.7 %collective-permute-start = (f32[544,128]{1,0:T(8,128)S(1)}, f32[544,128]{1,0:T(8,128)S(1)}, u32[]{:S(2)}, u32[]{:S(2)}) collective-permute-start(f32[544,128]{1,0:T(8,128)S(1)} %get-tuple-element.7), channel_id=1, source_target_pairs={{0,32},{32,0},{1,33},{33,1},{2,34},{34,2},{3,35},{35,3},{4,36},{36... | collective-permute-start | bytes 835592 | tf_op jit(solution)/shard_map/ppermute | solution.py:326
  13.8 1.2 %collective-permute-done = f32[544,128]{1,0:T(8,128)S(1)} collective-permute-done((f32[544,128]{1,0:T(8,128)S(1)}, f32[544,128]{1,0:T(8,128)S(1)}, u32[]{:S(2)}, u32[]{:S(2)}) %collective-permute-start) | collective-permute-done | bytes 278560 | tf_op jit(solution)/shard_map/ppermute | solution.py:326
  15.1 18.0 %all_to_all.15 = f32[32,17,128]{2,1,0:T(8,128)S(1)} all-to-all(f32[32,17,128]{2,1,0:T(8,128)S(1)} %reshape.33), channel_id=1, replica_groups=mesh['z'=8,'core'=2,'y'=8,'x'=4] {'y','x'}, dimensions={0} | all-to-all | bytes 557056 | tf_op jit(solution)/shard_map/all_to_all | solution.py:321
  33.1 17.4 %all_to_all.16 = f32[8,17,128]{2,1,0:T(8,128)S(1)} all-to-all(f32[8,17,128]{2,1,0:T(8,128)S(1)} %broadcast_in_dim.4), channel_id=1, replica_groups=mesh['z'=8,'core'=2,'y'=8,'x'=4] {'z'}, dimensions={0} | all-to-all | bytes 139264 | tf_op jit(solution)/shard_map/all_to_all | solution.py:321
  50.6 16.3 %all_to_all.17 = f32[32,17,128]{2,1,0:T(8,128)S(1)} all-to-all(f32[32,17,128]{2,1,0:T(8,128)S(1)} %broadcast_in_dim.5), channel_id=1, replica_groups=mesh['z'=8,'core'=2,'y'=8,'x'=4] {'y','x'}, dimensions={0} | all-to-all | bytes 557056 | tf_op jit(solution)/shard_map/all_to_all | solution.py:321
  67.0 7.2 %collective-permute-start.1 = (f32[544,128]{1,0:T(8,128)S(1)}, f32[544,128]{1,0:T(8,128)S(1)}, u32[]{:S(2)}, u32[]{:S(2)}) collective-permute-start(f32[544,128]{1,0:T(8,128)S(1)} %reshape.34.mine_ref), channel_id=1, source_target_pairs={{0,32},{32,0},{1,33},{33,1},{2,34},{34,2},{3,35},{35,3},{4,36},{36... | collective-permute-start | bytes 835592 | tf_op jit(solution)/shard_map/ppermute | solution.py:332
  74.2 1.2 %collective-permute-done.1.other_ref = f32[544,128]{1,0:T(8,128)S(1)} collective-permute-done((f32[544,128]{1,0:T(8,128)S(1)}, f32[544,128]{1,0:T(8,128)S(1)}, u32[]{:S(2)}, u32[]{:S(2)}) %collective-permute-start.1) | collective-permute-done | bytes 278560 | tf_op jit(solution)/shard_map/ppermute | solution.py:332
  75.3 20.8 %solve.1 = (f32[16,128]{1,0:T(8,128)}, f32[4,128]{1,0:T(4,128)}) custom-call(s32[1]{0:T(128)} %bitcast.core_ref, s32[1]{0:T(128)S(6)} %copy.10.count_ref, s32[4,16]{1,0:T(4,128)} %bitcast.12, bf16[2048,512]{1,0:T(8,128)(2,1)} %rows_hbm.3, f32[544,128]{1,0:T(8,128)S(1)} %reshape.34.mine_ref, f32[544,128]{1,0:T(8,128)S(1)} %collective-permute-done.1.other_ref, ...), custom_call_target="tpu_custom_call" | custom-call | tf_op jit(solution)/shard_map/solve/pallas_call | solution.py:300
  (7 shorter events, 0.2 us)
Async XLA Ops:
  5.1 9.9 %collective-permute-start = (f32[544,128]{1,0:T(8,128)S(1)}, f32[544,128]{1,0:T(8,128)S(1)}, u32[]{:S(2)}, u32[]{:S(2)}) collective-permute-start(f32[544,128]{1,0:T(8,128)S(1)} %get-tuple-element.7), channel_id=1, source_target_pairs={{0,32},{32,0},{1,33},{33,1},{2,34},{34,2},{3,35},{35,3},{4,36},{36... | collective-permute-start | bytes 835592 | tf_op jit(solution)/shard_map/ppermute | solution.py:326
  67.0 8.4 %collective-permute-start.1 = (f32[544,128]{1,0:T(8,128)S(1)}, f32[544,128]{1,0:T(8,128)S(1)}, u32[]{:S(2)}, u32[]{:S(2)}) collective-permute-start(f32[544,128]{1,0:T(8,128)S(1)} %reshape.34.mine_ref), channel_id=1, source_target_pairs={{0,32},{32,0},{1,33},{33,1},{2,34},{34,2},{3,35},{35,3},{4,36},{36... | collective-permute-start | bytes 835592 | tf_op jit(solution)/shard_map/ppermute | solution.py:332

commit v5 on v4

--- a/solution.py
+++ b/solution.py
@@ -138,16 +138,22 @@
             groups, sides = list(carry[: 8 - k]), list(carry[8 - k :])
             cols = [spread_lane(groups[0], start + j) for j in range(8)]
             panel, side = groups[0], sides[0]
-            for j in range(8):
-                here = sub == j
-                pivot = cols[j]
-                inverse = 1.0 / wide(pivot[j : j + 1, :])
-                row, side_row = wide(panel[j : j + 1, :]) * inverse, wide(side[j : j + 1, :]) * inverse
-                for c in range(j + 1, 8):
-                    entry = wide(cols[c][j : j + 1, :]) * inverse
-                    cols[c] = jnp.where(here, entry, cols[c] - pivot * entry)
-                panel = jnp.where(here, row, panel - pivot * row)
-                side = jnp.where(here, side_row, side - pivot * side_row)
+            for j in range(0, 8, 2):
+                one, two = cols[j], cols[j + 1]
+                a, b, c = wide(one[j : j + 1, :]), wide(two[j : j + 1, :]), wide(two[j + 1 : j + 2, :])
+                inverse = 1.0 / (a * c - b * b)
+                upper, lower_row = sub == j, sub == j + 1
+                both = upper | lower_row
+                by_first = jnp.where(upper, -c, jnp.where(lower_row, b, one * c - two * b)) * inverse
+                by_second = jnp.where(upper, b, jnp.where(lower_row, -a, two * a - one * b)) * inverse
+
+                def pivot(v):
+                    x, y = wide(v[j : j + 1, :]), wide(v[j + 1 : j + 2, :])
+                    return jnp.where(both, 0.0, v) - (by_first * x + by_second * y)
+
+                for i in range(j + 2, 8):
+                    cols[i] = pivot(cols[i])
+                panel, side = pivot(panel), pivot(side)
             spread = [wide(panel[j : j + 1, :]) for j in range(8)]
             spread_side = [wide(side[j : j + 1, :]) for j in range(8)]
             for i in range(1, 8 - k):

time: 96.6 us -> 95.2 us (0.986)
  Pallas kernels: 24.6 us -> 23.3 us
    pallas_call x1, Pallas kernels: 20.8 us -> 19.5 us  [solve(): pl.pallas_call(solve_kernel, out_shape=(jax.ShapeDtypeStruct((TILES, TILE...]
where the time goes in v5:
time: 95.2 us; the launch traced here: 94.8 us
  blocking collectives  51.8 us (54%)
  Pallas kernels  23.3 us (24%)
  starting transfers between devices  15.9 us (17%)
  waiting for transfers between devices  2.33 us (2%)
  between operations  1.34 us (1%)
    all_to_all x3, blocking collectives, exchange(): return lax.all_to_all(x, axes, split_axis=0, concat_axis=0, tiled=True)  51.8 us
    pallas_call x1, Pallas kernels, solve(): pl.pallas_call(solve_kernel, out_shape=(jax.ShapeDtypeStruct((TILES, TILE...  19.5 us
    ppermute x1, starting transfers between devices, reduce_all(): half = keep + lax.ppermute(give, 'core', swap)  8.73 us
    ppermute x1, starting transfers between devices, reduce_all(): return (half, lax.ppermute(half, 'core', swap))  7.2 us
    pallas_call x1, Pallas kernels, assemble(): pl.pallas_call(assemble_kernel, out_shape=(half, half), in_specs=[smem, s...  3.81 us
  transfers between devices with their start and end apart: 2, of which 2 were waited for; matrix products, arithmetic and copies ran while one was open for 0% of the time, Pallas kernels for 0%

profile of v5, /device:TPU:1, one launch (start us, length us, event | category | flops | bytes accessed | tf_op | source)
XLA Modules:
  0.0 94.8 jit_solution(2084294572093635007)
XLA Ops:
  1.3 3.8 %assemble.1 = (f32[544,128]{1,0:T(8,128)S(1)}, f32[544,128]{1,0:T(8,128)S(1)}) custom-call(s32[1]{0:T(128)} %bitcast.core_ref, s32[1]{0:T(128)S(6)} %copy.10.count_ref, s32[4,16]{1,0:T(4,128)} %bitcast.11, bf16[2048,512]{1,0:T(8,128)(2,1)} %rows_hbm.3, f32[16,128]{1,0:T(8,128)} %bitcast.7, f32[16,128]{1,0:T(8,128)} %bitcast.9), custom_call_target="tpu_custom_call" | custom-call | tf_op jit(solution)/shard_map/assemble/pallas_call | solution.py:103
  5.1 8.7 %collective-permute-start = (f32[544,128]{1,0:T(8,128)S(1)}, f32[544,128]{1,0:T(8,128)S(1)}, u32[]{:S(2)}, u32[]{:S(2)}) collective-permute-start(f32[544,128]{1,0:T(8,128)S(1)} %get-tuple-element.7), channel_id=1, source_target_pairs={{0,32},{32,0},{1,33},{33,1},{2,34},{34,2},{3,35},{35,3},{4,36},{36... | collective-permute-start | bytes 835592 | tf_op jit(solution)/shard_map/ppermute | solution.py:332
  13.8 1.2 %collective-permute-done = f32[544,128]{1,0:T(8,128)S(1)} collective-permute-done((f32[544,128]{1,0:T(8,128)S(1)}, f32[544,128]{1,0:T(8,128)S(1)}, u32[]{:S(2)}, u32[]{:S(2)}) %collective-permute-start) | collective-permute-done | bytes 278560 | tf_op jit(solution)/shard_map/ppermute | solution.py:332
  15.1 18.0 %all_to_all.15 = f32[32,17,128]{2,1,0:T(8,128)S(1)} all-to-all(f32[32,17,128]{2,1,0:T(8,128)S(1)} %reshape.33), channel_id=1, replica_groups=mesh['z'=8,'core'=2,'y'=8,'x'=4] {'y','x'}, dimensions={0} | all-to-all | bytes 557056 | tf_op jit(solution)/shard_map/all_to_all | solution.py:327
  33.1 17.4 %all_to_all.16 = f32[8,17,128]{2,1,0:T(8,128)S(1)} all-to-all(f32[8,17,128]{2,1,0:T(8,128)S(1)} %broadcast_in_dim.4), channel_id=1, replica_groups=mesh['z'=8,'core'=2,'y'=8,'x'=4] {'z'}, dimensions={0} | all-to-all | bytes 139264 | tf_op jit(solution)/shard_map/all_to_all | solution.py:327
  50.6 16.3 %all_to_all.17 = f32[32,17,128]{2,1,0:T(8,128)S(1)} all-to-all(f32[32,17,128]{2,1,0:T(8,128)S(1)} %broadcast_in_dim.5), channel_id=1, replica_groups=mesh['z'=8,'core'=2,'y'=8,'x'=4] {'y','x'}, dimensions={0} | all-to-all | bytes 557056 | tf_op jit(solution)/shard_map/all_to_all | solution.py:327
  67.0 7.2 %collective-permute-start.1 = (f32[544,128]{1,0:T(8,128)S(1)}, f32[544,128]{1,0:T(8,128)S(1)}, u32[]{:S(2)}, u32[]{:S(2)}) collective-permute-start(f32[544,128]{1,0:T(8,128)S(1)} %reshape.34.mine_ref), channel_id=1, source_target_pairs={{0,32},{32,0},{1,33},{33,1},{2,34},{34,2},{3,35},{35,3},{4,36},{36... | collective-permute-start | bytes 835592 | tf_op jit(solution)/shard_map/ppermute | solution.py:338
  74.2 1.2 %collective-permute-done.1.other_ref = f32[544,128]{1,0:T(8,128)S(1)} collective-permute-done((f32[544,128]{1,0:T(8,128)S(1)}, f32[544,128]{1,0:T(8,128)S(1)}, u32[]{:S(2)}, u32[]{:S(2)}) %collective-permute-start.1) | collective-permute-done | bytes 278560 | tf_op jit(solution)/shard_map/ppermute | solution.py:338
  75.3 19.5 %solve.1 = (f32[16,128]{1,0:T(8,128)}, f32[4,128]{1,0:T(4,128)}) custom-call(s32[1]{0:T(128)} %bitcast.core_ref, s32[1]{0:T(128)S(6)} %copy.10.count_ref, s32[4,16]{1,0:T(4,128)} %bitcast.12, bf16[2048,512]{1,0:T(8,128)(2,1)} %rows_hbm.3, f32[544,128]{1,0:T(8,128)S(1)} %reshape.34.mine_ref, f32[544,128]{1,0:T(8,128)S(1)} %collective-permute-done.1.other_ref, ...), custom_call_target="tpu_custom_call" | custom-call | tf_op jit(solution)/shard_map/solve/pallas_call | solution.py:306
  (7 shorter events, 0.2 us)
Async XLA Ops:
  5.1 9.9 %collective-permute-start = (f32[544,128]{1,0:T(8,128)S(1)}, f32[544,128]{1,0:T(8,128)S(1)}, u32[]{:S(2)}, u32[]{:S(2)}) collective-permute-start(f32[544,128]{1,0:T(8,128)S(1)} %get-tuple-element.7), channel_id=1, source_target_pairs={{0,32},{32,0},{1,33},{33,1},{2,34},{34,2},{3,35},{35,3},{4,36},{36... | collective-permute-start | bytes 835592 | tf_op jit(solution)/shard_map/ppermute | solution.py:332
  67.0 8.4 %collective-permute-start.1 = (f32[544,128]{1,0:T(8,128)S(1)}, f32[544,128]{1,0:T(8,128)S(1)}, u32[]{:S(2)}, u32[]{:S(2)}) collective-permute-start(f32[544,128]{1,0:T(8,128)S(1)} %reshape.34.mine_ref), channel_id=1, source_target_pairs={{0,32},{32,0},{1,33},{33,1},{2,34},{34,2},{3,35},{35,3},{4,36},{36... | collective-permute-start | bytes 835592 | tf_op jit(solution)/shard_map/ppermute | solution.py:338

commit v6 on v4

--- a/solution.py
+++ b/solution.py
@@ -127,39 +127,52 @@
     groups = [rows[8 * k : 8 * k + 8] for k in range(8)]
     sides = [(lane - first - 8 * k == sub).astype(F32) for k in range(8)]
     lower, scaled = [], []
-    for k in range(8):
-        start = first + 8 * k
-
+    def step(k, groups, sides):
+        groups, sides, start = list(groups), list(sides), first + 8 * k
+        cols = [spread_lane(groups[0], start + j) for j in range(8)]
+        panel, side = groups[0], sides[0]
+        for j in range(0, 8, 2):
+            one, two = cols[j], cols[j + 1]
+            a, b, c = wide(one[j : j + 1, :]), wide(two[j : j + 1, :]), wide(two[j + 1 : j + 2, :])
+            inverse = 1.0 / (a * c - b * b)
+            upper, lower_row = sub == j, sub == j + 1
+            both = upper | lower_row
+            by_first = jnp.where(upper, -c, jnp.where(lower_row, b, one * c - two * b)) * inverse
+            by_second = jnp.where(upper, b, jnp.where(lower_row, -a, two * a - one * b)) * inverse
+
+            def pivot(v):
+                x, y = wide(v[j : j + 1, :]), wide(v[j + 1 : j + 2, :])
+                return jnp.where(both, 0.0, v) - (by_first * x + by_second * y)
+
+            for i in range(j + 2, 8):
+                cols[i] = pivot(cols[i])
+            panel, side = pivot(panel), pivot(side)
+        spread = [wide(panel[j : j + 1, :]) for j in range(8)]
+        spread_side = [wide(side[j : j + 1, :]) for j in range(8)]
+        for i in range(1, len(groups)):
+            lead = [spread_lane(groups[i], start + j) for j in range(8)]
+            groups[i] = groups[i] - add_up([lead[j] * spread[j] for j in range(8)])
+            sides[i] = sides[i] - add_up([lead[j] * spread_side[j] for j in range(8)])
+        return groups[1:], sides[1:], side
+
+    for k in range(0, 8, 2):
         todo = tasks.pop(0) if tasks and k >= tasks[0][0] else None
+        more = tasks.pop(0) if tasks and k >= tasks[0][0] else None
 
         def body(_, carry):
-            if todo:
-                todo[1]()
-            groups, sides = list(carry[: 8 - k]), list(carry[8 - k :])
-            cols = [spread_lane(groups[0], start + j) for j in range(8)]
-            panel, side = groups[0], sides[0]
-            for j in range(8):
-                here = sub == j
-                pivot = cols[j]
-                inverse = 1.0 / wide(pivot[j : j + 1, :])
-                row, side_row = wide(panel[j : j + 1, :]) * inverse, wide(side[j : j + 1, :]) * inverse
-                for c in range(j + 1, 8):
-                    entry = wide(cols[c][j : j + 1, :]) * inverse
-                    cols[c] = jnp.where(here, entry, cols[c] - pivot * entry)
-                panel = jnp.where(here, row, panel - pivot * row)
-                side = jnp.where(here, side_row, side - pivot * side_row)
-            spread = [wide(panel[j : j + 1, :]) for j in range(8)]
-            spread_side = [wide(side[j : j + 1, :]) for j in range(8)]
-            for i in range(1, 8 - k):
-                lead = [spread_lane(groups[i], start + j) for j in range(8)]
-                groups[i] = groups[i] - add_up([lead[j] * spread[j] for j in range(8)])
-                sides[i] = sides[i] - add_up([lead[j] * spread_side[j] for j in range(8)])
-            return (*groups[1:], panel, *sides[1:], side)
+            for task in (todo, more):
+                if task:
+                    task[1]()
+            rest, others, one = step(k, carry[: 8 - k], carry[8 - k :])
+            after = others[0]
+            rest, others, two = step(k + 1, rest, others)
+            return (*rest, after, after, *others, one, two)
 
         lower.append(sides[0])
         carry = lax.fori_loop(0, once, body, (*groups, *sides))
-        groups, sides = list(carry[: 7 - k]), list(carry[8 - k : -1])
-        scaled.append(carry[-1])
+        lower.append(carry[6 - k])
+        groups, sides = list(carry[: 6 - k]), list(carry[8 - k : 14 - 2 * k])
+        scaled += carry[14 - 2 * k :]
     return jnp.concatenate(lower, axis=0), jnp.concatenate(scaled, axis=0)
 
 

time: 96.6 us -> 94.5 us (0.978)
  Pallas kernels: 24.6 us -> 22.6 us
    pallas_call x1, Pallas kernels: 20.8 us -> 18.7 us  [solve(): pl.pallas_call(solve_kernel, out_shape=(jax.ShapeDtypeStruct((TILES, TILE...]
where the time goes in v6:
time: 94.5 us; the launch traced here: 94.1 us
  blocking collectives  51.8 us (55%)
  Pallas kernels  22.6 us (24%)
  starting transfers between devices  15.9 us (17%)
  waiting for transfers between devices  2.33 us (2%)
  between operations  1.34 us (1%)
    all_to_all x3, blocking collectives, exchange(): return lax.all_to_all(x, axes, split_axis=0, concat_axis=0, tiled=True)  51.8 us
    pallas_call x1, Pallas kernels, solve(): pl.pallas_call(solve_kernel, out_shape=(jax.ShapeDtypeStruct((TILES, TILE...  18.7 us
    ppermute x1, starting transfers between devices, reduce_all(): half = keep + lax.ppermute(give, 'core', swap)  8.73 us
    ppermute x1, starting transfers between devices, reduce_all(): return (half, lax.ppermute(half, 'core', swap))  7.2 us
    pallas_call x1, Pallas kernels, assemble(): pl.pallas_call(assemble_kernel, out_shape=(half, half), in_specs=[smem, s...  3.81 us
  transfers between devices with their start and end apart: 2, of which 2 were waited for; matrix products, arithmetic and copies ran while one was open for 0% of the time, Pallas kernels for 0%

profile of v6, /device:TPU:1, one launch (start us, length us, event | category | flops | bytes accessed | tf_op | source)
XLA Modules:
  0.0 94.1 jit_solution(15985341120764185888)
XLA Ops:
  1.3 3.8 %assemble.1 = (f32[544,128]{1,0:T(8,128)S(1)}, f32[544,128]{1,0:T(8,128)S(1)}) custom-call(s32[1]{0:T(128)} %bitcast.core_ref, s32[1]{0:T(128)S(6)} %copy.10.count_ref, s32[4,16]{1,0:T(4,128)} %bitcast.11, bf16[2048,512]{1,0:T(8,128)(2,1)} %rows_hbm.3, f32[16,128]{1,0:T(8,128)} %bitcast.7, f32[16,128]{1,0:T(8,128)} %bitcast.9), custom_call_target="tpu_custom_call" | custom-call | tf_op jit(solution)/shard_map/assemble/pallas_call | solution.py:103
  5.1 8.7 %collective-permute-start = (f32[544,128]{1,0:T(8,128)S(1)}, f32[544,128]{1,0:T(8,128)S(1)}, u32[]{:S(2)}, u32[]{:S(2)}) collective-permute-start(f32[544,128]{1,0:T(8,128)S(1)} %get-tuple-element.7), channel_id=1, source_target_pairs={{0,32},{32,0},{1,33},{33,1},{2,34},{34,2},{3,35},{35,3},{4,36},{36... | collective-permute-start | bytes 835592 | tf_op jit(solution)/shard_map/ppermute | solution.py:339
  13.8 1.2 %collective-permute-done = f32[544,128]{1,0:T(8,128)S(1)} collective-permute-done((f32[544,128]{1,0:T(8,128)S(1)}, f32[544,128]{1,0:T(8,128)S(1)}, u32[]{:S(2)}, u32[]{:S(2)}) %collective-permute-start) | collective-permute-done | bytes 278560 | tf_op jit(solution)/shard_map/ppermute | solution.py:339
  15.1 18.0 %all_to_all.15 = f32[32,17,128]{2,1,0:T(8,128)S(1)} all-to-all(f32[32,17,128]{2,1,0:T(8,128)S(1)} %reshape.33), channel_id=1, replica_groups=mesh['z'=8,'core'=2,'y'=8,'x'=4] {'y','x'}, dimensions={0} | all-to-all | bytes 557056 | tf_op jit(solution)/shard_map/all_to_all | solution.py:334
  33.1 17.4 %all_to_all.16 = f32[8,17,128]{2,1,0:T(8,128)S(1)} all-to-all(f32[8,17,128]{2,1,0:T(8,128)S(1)} %broadcast_in_dim.4), channel_id=1, replica_groups=mesh['z'=8,'core'=2,'y'=8,'x'=4] {'z'}, dimensions={0} | all-to-all | bytes 139264 | tf_op jit(solution)/shard_map/all_to_all | solution.py:334
  50.6 16.3 %all_to_all.17 = f32[32,17,128]{2,1,0:T(8,128)S(1)} all-to-all(f32[32,17,128]{2,1,0:T(8,128)S(1)} %broadcast_in_dim.5), channel_id=1, replica_groups=mesh['z'=8,'core'=2,'y'=8,'x'=4] {'y','x'}, dimensions={0} | all-to-all | bytes 557056 | tf_op jit(solution)/shard_map/all_to_all | solution.py:334
  67.0 7.2 %collective-permute-start.1 = (f32[544,128]{1,0:T(8,128)S(1)}, f32[544,128]{1,0:T(8,128)S(1)}, u32[]{:S(2)}, u32[]{:S(2)}) collective-permute-start(f32[544,128]{1,0:T(8,128)S(1)} %reshape.34.mine_ref), channel_id=1, source_target_pairs={{0,32},{32,0},{1,33},{33,1},{2,34},{34,2},{3,35},{35,3},{4,36},{36... | collective-permute-start | bytes 835592 | tf_op jit(solution)/shard_map/ppermute | solution.py:345
  74.2 1.2 %collective-permute-done.1.other_ref = f32[544,128]{1,0:T(8,128)S(1)} collective-permute-done((f32[544,128]{1,0:T(8,128)S(1)}, f32[544,128]{1,0:T(8,128)S(1)}, u32[]{:S(2)}, u32[]{:S(2)}) %collective-permute-start.1) | collective-permute-done | bytes 278560 | tf_op jit(solution)/shard_map/ppermute | solution.py:345
  75.3 18.7 %solve.1 = (f32[16,128]{1,0:T(8,128)}, f32[4,128]{1,0:T(4,128)}) custom-call(s32[1]{0:T(128)} %bitcast.core_ref, s32[1]{0:T(128)S(6)} %copy.10.count_ref, s32[4,16]{1,0:T(4,128)} %bitcast.12, bf16[2048,512]{1,0:T(8,128)(2,1)} %rows_hbm.3, f32[544,128]{1,0:T(8,128)S(1)} %reshape.34.mine_ref, f32[544,128]{1,0:T(8,128)S(1)} %collective-permute-done.1.other_ref, ...), custom_call_target="tpu_custom_call" | custom-call | tf_op jit(solution)/shard_map/solve/pallas_call | solution.py:313
  (7 shorter events, 0.2 us)
Async XLA Ops:
  5.1 9.9 %collective-permute-start = (f32[544,128]{1,0:T(8,128)S(1)}, f32[544,128]{1,0:T(8,128)S(1)}, u32[]{:S(2)}, u32[]{:S(2)}) collective-permute-start(f32[544,128]{1,0:T(8,128)S(1)} %get-tuple-element.7), channel_id=1, source_target_pairs={{0,32},{32,0},{1,33},{33,1},{2,34},{34,2},{3,35},{35,3},{4,36},{36... | collective-permute-start | bytes 835592 | tf_op jit(solution)/shard_map/ppermute | solution.py:339
  67.0 8.4 %collective-permute-start.1 = (f32[544,128]{1,0:T(8,128)S(1)}, f32[544,128]{1,0:T(8,128)S(1)}, u32[]{:S(2)}, u32[]{:S(2)}) collective-permute-start(f32[544,128]{1,0:T(8,128)S(1)} %reshape.34.mine_ref), channel_id=1, source_target_pairs={{0,32},{32,0},{1,33},{33,1},{2,34},{34,2},{3,35},{35,3},{4,36},{36... | collective-permute-start | bytes 835592 | tf_op jit(solution)/shard_map/ppermute | solution.py:345
